TPU v7x, 512 devices: a whole 4x4x16 slice. The times are simulated.
512 devices in a mesh: layer: 16 (over z), row: 8 (over x, core), col: 4 (over y).
Axes of the slice: x: 4, y: 4, z: 16, core: 2. Of those that a mesh axis runs over, the one named last changes fastest.
Arguments:
- density: float32 [4096, 4096], P(('row', 'col'), 'layer'), as said below
- pattern: int32 [32, 32], replicated, may hold values from 0 to 1, as said below
Outputs:
- purified: float32 [4096, 4096], P(('row', 'col'), 'layer')
Inputs may be any that keep to these rules, and one draw needn't show every extreme that they name: pattern is symmetric, its diagonal is all ones. density is symmetric.
All inputs are finite; a program needn't handle non-finite values.
Results may differ from a plain program's by a relative error of at most 0.00013.
Values sent between devices are 32-bit elements; how exact they have to be, the bound alone decides.
No kernel may reach another device: no remote copies, remote signals or barrier semaphores. Data moves between devices by JAX's collectives and lax.ppermute only.
A program may use at most 64 MiB of HBM per device.

v0:
```python
import jax
import jax.numpy as jnp
from jax import lax
from jax.sharding import PartitionSpec as P

TILE = 128


def times_panel(left, panel):
    return lax.dot_general(
        left,
        panel,
        (((1,), (1,)), ((), ())),
        precision=lax.Precision.HIGHEST,
        preferred_element_type=jnp.float32,
    )


def on_device(density, pattern):
    row_count, col_count = density.shape
    tile_rows = row_count // TILE
    tile_cols = col_count // TILE
    row_start = lax.axis_index(("row", "col")) * tile_rows
    col_start = lax.axis_index("layer") * tile_cols
    local_keep = lax.dynamic_slice(pattern, (row_start, col_start), (tile_rows, tile_cols)).astype(
        jnp.float32
    )
    expanded = jnp.broadcast_to(
        local_keep[:, None, :, None], (tile_rows, TILE, tile_cols, TILE)
    ).reshape(row_count, col_count)
    masked = density * expanded
    gathered = lax.all_gather(masked, ("row", "col"), axis=0, tiled=True)
    partial_value = times_panel(masked, gathered)
    square = lax.psum_scatter(partial_value, "layer", scatter_dimension=1, tiled=True)
    cube_part = times_panel(square, gathered)
    cube = lax.psum_scatter(cube_part, "layer", scatter_dimension=1, tiled=True)
    return 3.0 * square - 2.0 * cube


def solution(mesh):
    return jax.shard_map(
        on_device,
        mesh=mesh,
        in_specs=(P(("row", "col"), "layer"), P()),
        out_specs=P(("row", "col"), "layer"),
        check_vma=False,
    )
```

profile of v0, /device:TPU:2, one launch (start us, length us, event | category | flops | bytes accessed | tf_op | source)
XLA Modules:
  0.0 245.6 jit_solution(10174428422946597006)
XLA Ops:
  6.5 0.0 all-gather.2.cloned.1.call-start
  6.5 0.8 convert_bitcast_fusion
  7.3 0.1 broadcast_bitcast_fusion
  7.4 1.6 broadcast_multiply_fusion
  8.9 0.0 all-gather.2.cloned.1.call-update
  9.0 0.0 reduce-scatter.3.cloned.1.call-start
  9.0 67.0 %all-gather.2.cloned.1.call-done = f32[4096,256]{1,0:T(8,128)} async-done(((f32[128,256]{1,0:T(8,128)}), f32[4096,256]{1,0:T(8,128)}) %all-gather.2.cloned.1.call-update) | async-done | bytes 4194320 | tf_op jit(solution)/shard_map/all_gather | solution.py:32
  76.0 7.9 %fusion = f32[128,4096]{1,0:T(8,128)} fusion(f32[128,256]{1,0:T(8,128)} %broadcast_multiply_fusion, f32[4096,256]{1,0:T(8,128)} %all-gather.2.cloned.1.call-done), kind=kOutput, calls=%fused_computation.4 | convolution fusion | flops 1610612736 | bytes 6422528 | tf_op jit(solution)/shard_map/dot_general | solution.py:10
  83.8 0.0 reduce-scatter.3.cloned.1.call-update
  83.9 0.0 reduce-scatter.5.cloned.1.call-start
  83.9 74.1 %reduce-scatter.3.cloned.1.call-done = f32[128,256]{1,0:T(8,128)} async-done(((f32[128,4096]{1,0:T(8,128)}), f32[128,256]{1,0:T(8,128)}) %reduce-scatter.3.cloned.1.call-update) | async-done | bytes 131088 | tf_op jit(solution)/shard_map/reduce_scatter | solution.py:34
  158.0 0.0 copy-start
  158.0 7.9 %fusion.1 = f32[128,4096]{1,0:T(8,128)} fusion(f32[128,256]{1,0:T(8,128)} %reduce-scatter.3.cloned.1.call-done, f32[4096,256]{1,0:T(8,128)} %all-gather.2.cloned.1.call-done), kind=kOutput, calls=%fused_computation.5 | convolution fusion | flops 1610612736 | bytes 6422528 | tf_op jit(solution)/shard_map/dot_general | solution.py:10
  165.9 0.0 reduce-scatter.5.cloned.1.call-update
  165.9 71.6 %reduce-scatter.5.cloned.1.call-done = f32[128,256]{1,0:T(8,128)} async-done(((f32[128,4096]{1,0:T(8,128)}), f32[128,256]{1,0:T(8,128)}) %reduce-scatter.5.cloned.1.call-update) | async-done | bytes 131088 | tf_op jit(solution)/shard_map/reduce_scatter | solution.py:36
  237.5 0.0 copy-done
  237.5 1.6 multiply_subtract_fusion
Async XLA Ops:
  6.5 69.5 %all-gather.2.cloned.1.call-start = ((), (), s32[]{:S(2)}) async-start(), calls=%async_computation.2 | async-start | bytes 4325376 | tf_op jit(solution)/shard_map/all_gather | solution.py:32
  9.0 149.1 %reduce-scatter.3.cloned.1.call-start = ((), (), s32[]{:S(2)}) async-start(), calls=%async_computation.3 | async-start | bytes 2228224 | tf_op jit(solution)/shard_map/reduce_scatter | solution.py:34
  83.9 153.7 %reduce-scatter.5.cloned.1.call-start = ((), (), s32[]{:S(2)}) async-start(), calls=%async_computation.4 | async-start | bytes 2228224 | tf_op jit(solution)/shard_map/reduce_scatter | solution.py:36
  158.0 79.5 %copy-start = (f32[128,256]{1,0:T(8,128)S(1)}, f32[128,256]{1,0:T(8,128)}, u32[]{:S(2)}) copy-start(f32[128,256]{1,0:T(8,128)} %reduce-scatter.3.cloned.1.call-done) | copy-start | bytes 393220
Sparse Core Ops, SparseCore 0:
  10.5 65.4 all-gather.1
  84.0 73.9 reduce-scatter.2
  166.1 71.4 reduce-scatter.4
where the time goes:
time: 246 us
  waiting for transfers between devices  213 us (87%)
  matrix products  15.7 us (6%)
  between operations  13.1 us (5%)
  other arithmetic  3.9 us (2%)
    reduce_scatter x1, waiting for transfers between devices, on_device(): lax.psum_scatter(partial_value, 'layer', scatter_dimension=1, tiled=True)  74.1 us
    reduce_scatter x1, waiting for transfers between devices, on_device(): cube = lax.psum_scatter(cube_part, 'layer', scatter_dimension=1, tiled=True)  71.6 us
    all_gather x1, waiting for transfers between devices, on_device(): gathered = lax.all_gather(masked, ('row', 'col'), axis=0, tiled=True)  67 us
    dot_general x2, matrix products, times_panel(): lax.dot_general(left, panel, (((1,), (1,)), ((), ())), precision=lax.Prec...  15.7 us
  transfers between devices with their start and end apart: 3, of which 3 were waited for; matrix products, arithmetic and copies ran while one was open for 0% of the time, Pallas kernels for 0%

commit v1 on v0

v1 whole, which is shorter than its diff:
```python
import jax
import jax.numpy as jnp
from jax import lax
from jax.experimental import pallas as pl
from jax.experimental.pallas import tpu as pltpu
from jax.sharding import Mesh
from jax.sharding import PartitionSpec as P


TILE = 128
LAYERS = 16
HALF = 8
DISTANCES = (0, -1, 1, -2, 2, -3, 3, -4)


VMEM = pl.BlockSpec(memory_space=pltpu.VMEM)


def shape(*dims):
    return jax.ShapeDtypeStruct(dims, jnp.float32)


def split(value):
    high = value.astype(jnp.bfloat16)
    low = (value - high.astype(jnp.float32)).astype(jnp.bfloat16)
    return high, low


def times(left, right):
    left_high, left_low = split(left)
    right_high, right_low = split(right)
    both = jnp.dot(
        jnp.concatenate([left_high, left_low], 0), right_high, preferred_element_type=jnp.float32
    )
    cross = jnp.dot(left_high, right_low, preferred_element_type=jnp.float32)
    return both[:TILE] + (both[TILE:] + cross)


def mask_kernel(density_ref, pattern_ref, out_ref):
    row = 8 * lax.axis_index("x") + 4 * lax.axis_index("c") + lax.axis_index("y")
    layer = lax.axis_index("z")
    for tile in range(2):
        keep = pattern_ref[row, 2 * layer + tile].astype(jnp.float32)
        columns = slice(TILE * tile, TILE * (tile + 1))
        out_ref[:, columns] = density_ref[:, columns] * keep


def mask(density, pattern):
    return pl.pallas_call(
        mask_kernel,
        out_shape=shape(TILE, 2 * TILE),
        in_specs=[VMEM, pl.BlockSpec(memory_space=pltpu.SMEM)],
        out_specs=VMEM,
        compiler_params=pltpu.CompilerParams(vmem_limit_bytes=4 << 20),
    )(density, pattern)


def square_kernel(*refs):
    lefts = refs[:HALF]
    mine_ref, other_ref, own_ref, away_ref, panel_ref = refs[HALF:]
    layer, core = lax.axis_index("z"), lax.axis_index("c")
    pair, parity = lax.div(layer, 2), lax.rem(layer, 2)
    for distance, left_ref in zip(DISTANCES, lefts, strict=True):
        panel_ref[lax.rem(pair + (distance + HALF), HALF)] = left_ref[...]
    own = away = jnp.zeros((TILE, 2 * TILE), jnp.float32)
    for block_ref, half in ((mine_ref, core), (other_ref, 1 - core)):
        for x in range(4):
            left = panel_ref[2 * x + half]
            near = block_ref[pl.ds(4 * x + 2 * parity, 2)].reshape(2 * TILE, 2 * TILE)
            far = block_ref[pl.ds(4 * x + 2 * (1 - parity), 2)].reshape(2 * TILE, 2 * TILE)
            own += times(left, near)
            away += times(left, far)
    own_ref[...] = own
    away_ref[...] = away


def square_call(lefts, mine, other):
    return pl.pallas_call(
        square_kernel,
        out_shape=(shape(TILE, 2 * TILE), shape(TILE, 2 * TILE), shape(HALF, TILE, 2 * TILE)),
        in_specs=[VMEM] * 10,
        out_specs=(VMEM, VMEM, VMEM),
        compiler_params=pltpu.CompilerParams(vmem_limit_bytes=16 << 20),
        cost_estimate=pl.CostEstimate(
            flops=6 * 128 * 2048 * 512, bytes_accessed=6 << 20, transcendentals=0
        ),
    )(*lefts, mine, other)


def cube_kernel(square_ref, here_ref, there_ref, mine_ref, other_ref, out_ref):
    core = lax.axis_index("c")
    parity = lax.rem(lax.axis_index("z"), 2)
    cube = jnp.zeros((TILE, 2 * TILE), jnp.float32)
    for block_ref, half in ((mine_ref, core), (other_ref, 1 - core)):
        for x in range(4):
            for panel_ref, which in ((here_ref, parity), (there_ref, 1 - parity)):
                right = block_ref[pl.ds(4 * x + 2 * which, 2)].reshape(2 * TILE, 2 * TILE)
                cube += times(panel_ref[2 * x + half], right)
    out_ref[...] = 3.0 * square_ref[...] - 2.0 * cube


def cube_call(*operands):
    return pl.pallas_call(
        cube_kernel,
        out_shape=shape(TILE, 2 * TILE),
        in_specs=[VMEM] * 5,
        out_specs=VMEM,
        compiler_params=pltpu.CompilerParams(vmem_limit_bytes=16 << 20),
        cost_estimate=pl.CostEstimate(
            flops=6 * 128 * 4096 * 256, bytes_accessed=6 << 20, transcendentals=0
        ),
    )(*operands)


def ring(block):
    up = [(z, (z + 2) % LAYERS) for z in range(LAYERS)]
    down = [(z, (z - 2) % LAYERS) for z in range(LAYERS)]
    blocks = [block]
    ahead = behind = block
    for _ in range(1, 4):
        ahead = lax.ppermute(ahead, "z", up)
        behind = lax.ppermute(behind, "z", down)
        blocks += [ahead, behind]
    blocks.append(lax.ppermute(ahead, "z", up))
    return blocks


def to_plane(block):
    copies = jnp.broadcast_to(block[None], (16, *block.shape))
    return lax.all_to_all(copies, ("x", "y"), 0, 0)


CORES = [(0, 1), (1, 0)]
NEIGHBOURS = [(z, z ^ 1) for z in range(LAYERS)]
SWAP = [
    (4 * z + y, 4 * (z ^ 1) + (y ^ 2))
    for z in range(LAYERS)
    for y in range(4)
    if z % 2 != y // 2
]


def on_device(density, pattern):
    matched = lax.rem(lax.axis_index("z"), 2) == lax.div(lax.axis_index("y"), 2)
    masked = mask(density, pattern)
    moved = lax.ppermute(masked, ("z", "y"), SWAP)
    lefts = ring(masked)
    mine = to_plane(jnp.where(matched, masked, moved))
    other = lax.ppermute(mine, "c", CORES)
    own, away, here = square_call(lefts, mine, other)
    square = own + lax.ppermute(away, "z", NEIGHBOURS)
    there = lax.ppermute(here, "z", NEIGHBOURS)
    mine = to_plane(square)
    other = lax.ppermute(mine, "c", CORES)
    return cube_call(square, here, there, mine, other)


def solution(mesh):
    split_mesh = Mesh(mesh.devices.reshape(LAYERS, 4, 2, 4), ("z", "x", "c", "y"))
    return jax.shard_map(
        on_device,
        mesh=split_mesh,
        in_specs=(P(("x", "c", "y"), "z"), P()),
        out_specs=P(("x", "c", "y"), "z"),
        check_vma=False,
    )
```

time: 246 us -> 165 us (0.67)
  the two profiles are of different devices: /device:TPU:2 before, /device:TPU:1 now
where the time goes in v1:
time: 165 us
  blocking collectives  68.7 us (42%)
  starting transfers between devices  53.4 us (32%)
  waiting for transfers between devices  36.5 us (22%)
  Pallas kernels  3.82 us (2%)
  local copies, waits for them, and re-layouts  2.01 us (1%)
    all_to_all x2, blocking collectives, to_plane(): return lax.all_to_all(copies, ('x', 'y'), 0, 0)  68.7 us
    ppermute x1, waiting for transfers between devices, on_device(): there = lax.ppermute(here, 'z', NEIGHBOURS)  23.4 us
    ppermute x3, starting transfers between devices, ring(): behind = lax.ppermute(behind, 'z', down)  18.6 us
    ppermute x2, starting transfers between devices, on_device(): other = lax.ppermute(mine, 'c', CORES)  11.8 us
    ppermute x3, starting transfers between devices, ring(): ahead = lax.ppermute(ahead, 'z', up)  9.65 us
    ppermute x3, waiting for transfers between devices, ring(): ahead = lax.ppermute(ahead, 'z', up)  6.45 us
    ppermute x1, starting transfers between devices, on_device(): square = own + lax.ppermute(away, 'z', NEIGHBOURS)  4.62 us
    ppermute x1, starting transfers between devices, ring(): blocks.append(lax.ppermute(ahead, 'z', up))  4.51 us
  transfers between devices with their start and end apart: 12, of which 7 were waited for; matrix products, arithmetic and copies ran while one was open for 0% of the time, Pallas kernels for 0%

profile of v1, /device:TPU:1, one launch (start us, length us, event | category | flops | bytes accessed | tf_op | source)
XLA Modules:
  0.0 164.6 jit_solution(3126250650993697662)
XLA Ops:
  0.0 0.0 copy-start
  0.0 0.9 copy-done
  0.9 0.0 copy-start.1
  0.9 0.7 copy-done.1
  1.6 0.8 shard_map.28.refs_0_
  2.5 0.7 collective-permute-start.7
  3.1 0.0 collective-permute-done.7
  3.2 0.2 broadcast_in_dim.4
  3.4 41.4 %all_to_all.10.refs_8_ = f32[16,128,256]{2,1,0:T(8,128)S(1)} all-to-all(f32[16,128,256]{2,1,0:T(8,128)S(1)} %broadcast_in_dim.4), channel_id=1, replica_groups=mesh['z'=16,'x'=4,'c'=2,'y'=4] {'x','y'}, dimensions={0} | all-to-all | bytes 4194304 | tf_op jit(solution)/shard_map/all_to_all | solution.py:130
  44.8 5.1 %collective-permute-start.8 = (f32[16,128,256]{2,1,0:T(8,128)S(1)}, f32[16,128,256]{2,1,0:T(8,128)S(1)}, u32[]{:S(2)}, u32[]{:S(2)}) collective-permute-start(f32[16,128,256]{2,1,0:T(8,128)S(1)} %all_to_all.10.refs_8_), channel_id=1, source_target_pairs={{0,4},{4,0},{1,5},{5,1},{2,6},{6,2},{3,7},{7,3},{8,12},{12,8},{9,1... | collective-permute-start | bytes 6291464 | tf_op jit(solution)/shard_map/ppermute | solution.py:149
  49.9 4.9 %collective-permute-start = (f32[128,256]{1,0:T(8,128)S(1)}, f32[128,256]{1,0:T(8,128)S(1)}, u32[]{:S(2)}, u32[]{:S(2)}) collective-permute-start(f32[128,256]{1,0:T(8,128)S(1)} %shard_map.28.refs_0_), channel_id=1, source_target_pairs={{0,64},{32,96},{64,128},{96,160},{128,192},{160,224},{192,256},{22... | collective-permute-start | bytes 393224 | tf_op jit(solution)/shard_map/ppermute | solution.py:121
  54.9 8.6 %collective-permute-start.1 = (f32[128,256]{1,0:T(8,128)S(1)}, f32[128,256]{1,0:T(8,128)S(1)}, u32[]{:S(2)}, u32[]{:S(2)}) collective-permute-start(f32[128,256]{1,0:T(8,128)S(1)} %shard_map.28.refs_0_), channel_id=1, source_target_pairs={{0,448},{32,480},{64,0},{96,32},{128,64},{160,96},{192,128},{224,1... | collective-permute-start | bytes 393224 | tf_op jit(solution)/shard_map/ppermute | solution.py:122
  63.4 4.8 %collective-permute-done.refs_1_ = f32[128,256]{1,0:T(8,128)S(1)} collective-permute-done((f32[128,256]{1,0:T(8,128)S(1)}, f32[128,256]{1,0:T(8,128)S(1)}, u32[]{:S(2)}, u32[]{:S(2)}) %collective-permute-start) | collective-permute-done | bytes 131104 | tf_op jit(solution)/shard_map/ppermute | solution.py:121
  68.3 1.9 %collective-permute-start.2 = (f32[128,256]{1,0:T(8,128)S(1)}, f32[128,256]{1,0:T(8,128)S(1)}, u32[]{:S(2)}, u32[]{:S(2)}) collective-permute-start(f32[128,256]{1,0:T(8,128)S(1)} %collective-permute-done.refs_1_), channel_id=1, source_target_pairs={{0,64},{32,96},{64,128},{96,160},{128,192},{160,224},{192,256},{22... | collective-permute-start | bytes 393224 | tf_op jit(solution)/shard_map/ppermute | solution.py:121
  70.2 0.0 collective-permute-done.1.refs_2_
  70.2 5.5 %collective-permute-start.3 = (f32[128,256]{1,0:T(8,128)S(1)}, f32[128,256]{1,0:T(8,128)S(1)}, u32[]{:S(2)}, u32[]{:S(2)}) collective-permute-start(f32[128,256]{1,0:T(8,128)S(1)} %collective-permute-done.1.refs_2_), channel_id=1, source_target_pairs={{0,448},{32,480},{64,0},{96,32},{128,64},{160,96},{192,128},{224,1... | collective-permute-start | bytes 393224 | tf_op jit(solution)/shard_map/ppermute | solution.py:122
  75.7 1.1 collective-permute-done.2.refs_3_
  76.8 2.8 %collective-permute-start.4 = (f32[128,256]{1,0:T(8,128)S(1)}, f32[128,256]{1,0:T(8,128)S(1)}, u32[]{:S(2)}, u32[]{:S(2)}) collective-permute-start(f32[128,256]{1,0:T(8,128)S(1)} %collective-permute-done.2.refs_3_), channel_id=1, source_target_pairs={{0,64},{32,96},{64,128},{96,160},{128,192},{160,224},{192,256},{22... | collective-permute-start | bytes 393224 | tf_op jit(solution)/shard_map/ppermute | solution.py:121
  79.6 0.0 collective-permute-done.3.refs_4_
  79.7 4.5 %collective-permute-start.5 = (f32[128,256]{1,0:T(8,128)S(1)}, f32[128,256]{1,0:T(8,128)S(1)}, u32[]{:S(2)}, u32[]{:S(2)}) collective-permute-start(f32[128,256]{1,0:T(8,128)S(1)} %collective-permute-done.3.refs_4_), channel_id=1, source_target_pairs={{0,448},{32,480},{64,0},{96,32},{128,64},{160,96},{192,128},{224,1... | collective-permute-start | bytes 393224 | tf_op jit(solution)/shard_map/ppermute | solution.py:122
  84.2 0.5 collective-permute-done.4.refs_5_
  84.7 4.5 %collective-permute-start.6 = (f32[128,256]{1,0:T(8,128)S(1)}, f32[128,256]{1,0:T(8,128)S(1)}, u32[]{:S(2)}, u32[]{:S(2)}) collective-permute-start(f32[128,256]{1,0:T(8,128)S(1)} %collective-permute-done.4.refs_5_), channel_id=1, source_target_pairs={{0,64},{32,96},{64,128},{96,160},{128,192},{160,224},{192,256},{22... | collective-permute-start | bytes 393224 | tf_op jit(solution)/shard_map/ppermute | solution.py:124
  89.2 1.3 collective-permute-done.5.refs_6_
  90.5 3.0 %collective-permute-done.6.refs_7_ = f32[128,256]{1,0:T(8,128)S(1)} collective-permute-done((f32[128,256]{1,0:T(8,128)S(1)}, f32[128,256]{1,0:T(8,128)S(1)}, u32[]{:S(2)}, u32[]{:S(2)}) %collective-permute-start.6) | collective-permute-done | bytes 131104 | tf_op jit(solution)/shard_map/ppermute | solution.py:124
  93.5 0.0 collective-permute-done.8.refs_9_
  93.5 1.3 shard_map.29
  94.7 4.6 %collective-permute-start.9 = (f32[128,256]{1,0:T(8,128)S(1)}, f32[128,256]{1,0:T(8,128)S(1)}, u32[]{:S(2)}, u32[]{:S(2)}) collective-permute-start(f32[128,256]{1,0:T(8,128)S(1)} %get-tuple-element.9), channel_id=1, source_target_pairs={{0,32},{32,0},{64,96},{96,64},{128,160},{160,128},{192,224},{224,1... | collective-permute-start | bytes 393224 | tf_op jit(solution)/shard_map/ppermute | solution.py:151
  99.4 2.3 %collective-permute-done.9 = f32[128,256]{1,0:T(8,128)S(1)} collective-permute-done((f32[128,256]{1,0:T(8,128)S(1)}, f32[128,256]{1,0:T(8,128)S(1)}, u32[]{:S(2)}, u32[]{:S(2)}) %collective-permute-start.9) | collective-permute-done | bytes 131104 | tf_op jit(solution)/shard_map/ppermute | solution.py:151
  101.7 0.2 broadcast_in_dim.5
  101.9 27.3 %all_to_all.11.mine_ref = f32[16,128,256]{2,1,0:T(8,128)S(1)} all-to-all(f32[16,128,256]{2,1,0:T(8,128)S(1)} %broadcast_in_dim.5), channel_id=1, replica_groups=mesh['z'=16,'x'=4,'c'=2,'y'=4] {'x','y'}, dimensions={0} | all-to-all | bytes 4194304 | tf_op jit(solution)/shard_map/all_to_all | solution.py:130
  129.2 6.7 %collective-permute-start.11 = (f32[16,128,256]{2,1,0:T(8,128)S(1)}, f32[16,128,256]{2,1,0:T(8,128)S(1)}, u32[]{:S(2)}, u32[]{:S(2)}) collective-permute-start(f32[16,128,256]{2,1,0:T(8,128)S(1)} %all_to_all.11.mine_ref), channel_id=1, source_target_pairs={{0,4},{4,0},{1,5},{5,1},{2,6},{6,2},{3,7},{7,3},{8,12},{12,8},{9,1... | collective-permute-start | bytes 6291464 | tf_op jit(solution)/shard_map/ppermute | solution.py:154
  135.9 3.5 %collective-permute-start.10 = (f32[8,128,256]{2,1,0:T(8,128)S(1)}, f32[8,128,256]{2,1,0:T(8,128)S(1)}, u32[]{:S(2)}, u32[]{:S(2)}) collective-permute-start(f32[8,128,256]{2,1,0:T(8,128)S(1)} %get-tuple-element.10.here_ref), channel_id=1, source_target_pairs={{0,32},{32,0},{64,96},{96,64},{128,160},{160,128},{192,224},{224,1... | collective-permute-start | bytes 3145736 | tf_op jit(solution)/shard_map/ppermute | solution.py:152
  139.5 23.4 %collective-permute-done.10.there_ref = f32[8,128,256]{2,1,0:T(8,128)S(1)} collective-permute-done((f32[8,128,256]{2,1,0:T(8,128)S(1)}, f32[8,128,256]{2,1,0:T(8,128)S(1)}, u32[]{:S(2)}, u32[]{:S(2)}) %collective-permute-start.10) | collective-permute-done | bytes 1048608 | tf_op jit(solution)/shard_map/ppermute | solution.py:152
  162.9 0.0 collective-permute-done.11.other_ref
  162.9 1.7 %shard_map.30 = f32[128,256]{1,0:T(8,128)} custom-call(f32[128,256]{1,0:T(8,128)S(1)} %add.3.square_ref, f32[8,128,256]{2,1,0:T(8,128)S(1)} %get-tuple-element.10.here_ref, f32[8,128,256]{2,1,0:T(8,128)S(1)} %collective-permute-done.10.there_ref, f32[16,128,256]{2,1,0:T(8,128)S(1)} %all_to_all.11.mine_ref, f32[16,128,256]{2,1,0:T(8,128)S(1)} %collective-permute-done.11.other_ref), custom_call_target="tpu_custom_call" | custom-call | flops 805306368 | bytes 6291456 | tf_op jit(solution)/shard_map/pallas_call | solution.py:103
  (2 shorter events, 0.0 us)
Async XLA Ops:
  0.0 0.9 copy-start
  0.9 0.7 copy-start.1
  2.5 0.7 collective-permute-start.7
  44.8 48.7 %collective-permute-start.8 = (f32[16,128,256]{2,1,0:T(8,128)S(1)}, f32[16,128,256]{2,1,0:T(8,128)S(1)}, u32[]{:S(2)}, u32[]{:S(2)}) collective-permute-start(f32[16,128,256]{2,1,0:T(8,128)S(1)} %all_to_all.10.refs_8_), channel_id=1, source_target_pairs={{0,4},{4,0},{1,5},{5,1},{2,6},{6,2},{3,7},{7,3},{8,12},{12,8},{9,1... | collective-permute-start | bytes 6291464 | tf_op jit(solution)/shard_map/ppermute | solution.py:149
  49.9 18.3 %collective-permute-start = (f32[128,256]{1,0:T(8,128)S(1)}, f32[128,256]{1,0:T(8,128)S(1)}, u32[]{:S(2)}, u32[]{:S(2)}) collective-permute-start(f32[128,256]{1,0:T(8,128)S(1)} %shard_map.28.refs_0_), channel_id=1, source_target_pairs={{0,64},{32,96},{64,128},{96,160},{128,192},{160,224},{192,256},{22... | collective-permute-start | bytes 393224 | tf_op jit(solution)/shard_map/ppermute | solution.py:121
  54.9 15.3 %collective-permute-start.1 = (f32[128,256]{1,0:T(8,128)S(1)}, f32[128,256]{1,0:T(8,128)S(1)}, u32[]{:S(2)}, u32[]{:S(2)}) collective-permute-start(f32[128,256]{1,0:T(8,128)S(1)} %shard_map.28.refs_0_), channel_id=1, source_target_pairs={{0,448},{32,480},{64,0},{96,32},{128,64},{160,96},{192,128},{224,1... | collective-permute-start | bytes 393224 | tf_op jit(solution)/shard_map/ppermute | solution.py:122
  68.3 8.5 %collective-permute-start.2 = (f32[128,256]{1,0:T(8,128)S(1)}, f32[128,256]{1,0:T(8,128)S(1)}, u32[]{:S(2)}, u32[]{:S(2)}) collective-permute-start(f32[128,256]{1,0:T(8,128)S(1)} %collective-permute-done.refs_1_), channel_id=1, source_target_pairs={{0,64},{32,96},{64,128},{96,160},{128,192},{160,224},{192,256},{22... | collective-permute-start | bytes 393224 | tf_op jit(solution)/shard_map/ppermute | solution.py:121
  70.2 9.5 %collective-permute-start.3 = (f32[128,256]{1,0:T(8,128)S(1)}, f32[128,256]{1,0:T(8,128)S(1)}, u32[]{:S(2)}, u32[]{:S(2)}) collective-permute-start(f32[128,256]{1,0:T(8,128)S(1)} %collective-permute-done.1.refs_2_), channel_id=1, source_target_pairs={{0,448},{32,480},{64,0},{96,32},{128,64},{160,96},{192,128},{224,1... | collective-permute-start | bytes 393224 | tf_op jit(solution)/shard_map/ppermute | solution.py:122
  76.8 7.9 %collective-permute-start.4 = (f32[128,256]{1,0:T(8,128)S(1)}, f32[128,256]{1,0:T(8,128)S(1)}, u32[]{:S(2)}, u32[]{:S(2)}) collective-permute-start(f32[128,256]{1,0:T(8,128)S(1)} %collective-permute-done.2.refs_3_), channel_id=1, source_target_pairs={{0,64},{32,96},{64,128},{96,160},{128,192},{160,224},{192,256},{22... | collective-permute-start | bytes 393224 | tf_op jit(solution)/shard_map/ppermute | solution.py:121
  79.7 10.9 %collective-permute-start.5 = (f32[128,256]{1,0:T(8,128)S(1)}, f32[128,256]{1,0:T(8,128)S(1)}, u32[]{:S(2)}, u32[]{:S(2)}) collective-permute-start(f32[128,256]{1,0:T(8,128)S(1)} %collective-permute-done.3.refs_4_), channel_id=1, source_target_pairs={{0,448},{32,480},{64,0},{96,32},{128,64},{160,96},{192,128},{224,1... | collective-permute-start | bytes 393224 | tf_op jit(solution)/shard_map/ppermute | solution.py:122
  84.7 8.8 %collective-permute-start.6 = (f32[128,256]{1,0:T(8,128)S(1)}, f32[128,256]{1,0:T(8,128)S(1)}, u32[]{:S(2)}, u32[]{:S(2)}) collective-permute-start(f32[128,256]{1,0:T(8,128)S(1)} %collective-permute-done.4.refs_5_), channel_id=1, source_target_pairs={{0,64},{32,96},{64,128},{96,160},{128,192},{160,224},{192,256},{22... | collective-permute-start | bytes 393224 | tf_op jit(solution)/shard_map/ppermute | solution.py:124
  94.7 7.0 %collective-permute-start.9 = (f32[128,256]{1,0:T(8,128)S(1)}, f32[128,256]{1,0:T(8,128)S(1)}, u32[]{:S(2)}, u32[]{:S(2)}) collective-permute-start(f32[128,256]{1,0:T(8,128)S(1)} %get-tuple-element.9), channel_id=1, source_target_pairs={{0,32},{32,0},{64,96},{96,64},{128,160},{160,128},{192,224},{224,1... | collective-permute-start | bytes 393224 | tf_op jit(solution)/shard_map/ppermute | solution.py:151
  129.2 33.7 %collective-permute-start.11 = (f32[16,128,256]{2,1,0:T(8,128)S(1)}, f32[16,128,256]{2,1,0:T(8,128)S(1)}, u32[]{:S(2)}, u32[]{:S(2)}) collective-permute-start(f32[16,128,256]{2,1,0:T(8,128)S(1)} %all_to_all.11.mine_ref), channel_id=1, source_target_pairs={{0,4},{4,0},{1,5},{5,1},{2,6},{6,2},{3,7},{7,3},{8,12},{12,8},{9,1... | collective-permute-start | bytes 6291464 | tf_op jit(solution)/shard_map/ppermute | solution.py:154
  135.9 26.9 %collective-permute-start.10 = (f32[8,128,256]{2,1,0:T(8,128)S(1)}, f32[8,128,256]{2,1,0:T(8,128)S(1)}, u32[]{:S(2)}, u32[]{:S(2)}) collective-permute-start(f32[8,128,256]{2,1,0:T(8,128)S(1)} %get-tuple-element.10.here_ref), channel_id=1, source_target_pairs={{0,32},{32,0},{64,96},{96,64},{128,160},{160,128},{192,224},{224,1... | collective-permute-start | bytes 3145736 | tf_op jit(solution)/shard_map/ppermute | solution.py:152

commit v2 on v1

--- a/solution.py
+++ b/solution.py
@@ -36,22 +36,34 @@
     return both[:TILE] + (both[TILE:] + cross)
 
 
-def mask_kernel(density_ref, pattern_ref, out_ref):
+def mask_kernel(density_hbm, pattern_hbm, out_ref, density_ref, pattern_ref, sems):
+    fetch_pattern = pltpu.make_async_copy(pattern_hbm, pattern_ref, sems.at[0])
+    fetch_density = pltpu.make_async_copy(density_hbm, density_ref, sems.at[1])
+    fetch_pattern.start()
+    fetch_density.start()
     row = 8 * lax.axis_index("x") + 4 * lax.axis_index("c") + lax.axis_index("y")
     layer = lax.axis_index("z")
+    fetch_pattern.wait()
+    keeps = [pattern_ref[row, 2 * layer + tile].astype(jnp.float32) for tile in range(2)]
+    fetch_density.wait()
     for tile in range(2):
-        keep = pattern_ref[row, 2 * layer + tile].astype(jnp.float32)
         columns = slice(TILE * tile, TILE * (tile + 1))
-        out_ref[:, columns] = density_ref[:, columns] * keep
+        out_ref[:, columns] = density_ref[:, columns] * keeps[tile]
 
 
 def mask(density, pattern):
+    hbm = pl.BlockSpec(memory_space=pltpu.HBM)
     return pl.pallas_call(
         mask_kernel,
         out_shape=shape(TILE, 2 * TILE),
-        in_specs=[VMEM, pl.BlockSpec(memory_space=pltpu.SMEM)],
+        in_specs=[hbm, hbm],
         out_specs=VMEM,
-        compiler_params=pltpu.CompilerParams(vmem_limit_bytes=4 << 20),
+        scratch_shapes=[
+            pltpu.VMEM(density.shape, jnp.float32),
+            pltpu.SMEM(pattern.shape, jnp.int32),
+            pltpu.SemaphoreType.DMA((2,)),
+        ],
+        compiler_params=pltpu.CompilerParams(vmem_limit_bytes=66_900_000),
     )(density, pattern)
 
 
@@ -125,8 +137,11 @@
     return blocks
 
 
-def to_plane(block):
-    copies = jnp.broadcast_to(block[None], (16, *block.shape))
+def spread(block):
+    return jnp.broadcast_to(block[None], (16, *block.shape))
+
+
+def to_plane(copies):
     return lax.all_to_all(copies, ("x", "y"), 0, 0)
 
 
@@ -145,12 +160,12 @@
     masked = mask(density, pattern)
     moved = lax.ppermute(masked, ("z", "y"), SWAP)
     lefts = ring(masked)
-    mine = to_plane(jnp.where(matched, masked, moved))
+    mine = to_plane(spread(jnp.where(matched, masked, moved)))
     other = lax.ppermute(mine, "c", CORES)
     own, away, here = square_call(lefts, mine, other)
     square = own + lax.ppermute(away, "z", NEIGHBOURS)
     there = lax.ppermute(here, "z", NEIGHBOURS)
-    mine = to_plane(square)
+    mine = to_plane(spread(square))
     other = lax.ppermute(mine, "c", CORES)
     return cube_call(square, here, there, mine, other)
 

time: 165 us -> 165 us (level)
  no operation moved by 1% of the time
where the time goes in v2:
time: 165 us; the launch traced here: 164 us
  blocking collectives  68.1 us (41%)
  starting transfers between devices  53.4 us (32%)
  waiting for transfers between devices  36.5 us (22%)
  Pallas kernels  4.59 us (3%)
    all_to_all x2, blocking collectives, to_plane(): return lax.all_to_all(copies, ('x', 'y'), 0, 0)  68.1 us
    ppermute x1, waiting for transfers between devices, on_device(): there = lax.ppermute(here, 'z', NEIGHBOURS)  23.4 us
    ppermute x3, starting transfers between devices, ring(): behind = lax.ppermute(behind, 'z', down)  18.6 us
    ppermute x2, starting transfers between devices, on_device(): other = lax.ppermute(mine, 'c', CORES)  11.8 us
    ppermute x3, starting transfers between devices, ring(): ahead = lax.ppermute(ahead, 'z', up)  9.65 us
    ppermute x3, waiting for transfers between devices, ring(): ahead = lax.ppermute(ahead, 'z', up)  6.45 us
    ppermute x1, starting transfers between devices, on_device(): square = own + lax.ppermute(away, 'z', NEIGHBOURS)  4.62 us
    ppermute x1, starting transfers between devices, ring(): blocks.append(lax.ppermute(ahead, 'z', up))  4.51 us
  transfers between devices with their start and end apart: 12, of which 7 were waited for; matrix products, arithmetic and copies ran while one was open for 0% of the time, Pallas kernels for 0%

profile of v2, /device:TPU:1, one launch (start us, length us, event | category | flops | bytes accessed | tf_op | source)
XLA Modules:
  0.0 164.1 jit_solution(9934998988551209154)
XLA Ops:
  0.0 1.6 shard_map.28.refs_0_
  1.6 0.7 collective-permute-start.7
  2.3 0.0 collective-permute-done.7
  2.3 0.9 broadcast_select_fusion
  3.2 0.2 broadcast_in_dim.4
  3.5 0.0 copy-start
  3.5 40.9 %all_to_all.10.refs_8_ = f32[16,128,256]{2,1,0:T(8,128)S(1)} all-to-all(f32[16,128,256]{2,1,0:T(8,128)S(1)} %broadcast_in_dim.4), channel_id=1, replica_groups=mesh['z'=16,'x'=4,'c'=2,'y'=4] {'x','y'}, dimensions={0} | all-to-all | bytes 4194304 | tf_op jit(solution)/shard_map/all_to_all | solution.py:145
  44.3 5.1 %collective-permute-start.8 = (f32[16,128,256]{2,1,0:T(8,128)S(1)}, f32[16,128,256]{2,1,0:T(8,128)S(1)}, u32[]{:S(2)}, u32[]{:S(2)}) collective-permute-start(f32[16,128,256]{2,1,0:T(8,128)S(1)} %all_to_all.10.refs_8_), channel_id=1, source_target_pairs={{0,4},{4,0},{1,5},{5,1},{2,6},{6,2},{3,7},{7,3},{8,12},{12,8},{9,1... | collective-permute-start | bytes 6291464 | tf_op jit(solution)/shard_map/ppermute | solution.py:164
  49.5 0.0 copy-done
  49.5 4.9 %collective-permute-start = (f32[128,256]{1,0:T(8,128)S(1)}, f32[128,256]{1,0:T(8,128)S(1)}, u32[]{:S(2)}, u32[]{:S(2)}) collective-permute-start(f32[128,256]{1,0:T(8,128)S(1)} %copy-done), channel_id=1, source_target_pairs={{0,64},{32,96},{64,128},{96,160},{128,192},{160,224},{192,256},{22... | collective-permute-start | bytes 393224 | tf_op jit(solution)/shard_map/ppermute | solution.py:133
  54.4 8.6 %collective-permute-start.1 = (f32[128,256]{1,0:T(8,128)S(1)}, f32[128,256]{1,0:T(8,128)S(1)}, u32[]{:S(2)}, u32[]{:S(2)}) collective-permute-start(f32[128,256]{1,0:T(8,128)S(1)} %copy-done), channel_id=1, source_target_pairs={{0,448},{32,480},{64,0},{96,32},{128,64},{160,96},{192,128},{224,1... | collective-permute-start | bytes 393224 | tf_op jit(solution)/shard_map/ppermute | solution.py:134
  63.0 4.8 %collective-permute-done.refs_1_ = f32[128,256]{1,0:T(8,128)S(1)} collective-permute-done((f32[128,256]{1,0:T(8,128)S(1)}, f32[128,256]{1,0:T(8,128)S(1)}, u32[]{:S(2)}, u32[]{:S(2)}) %collective-permute-start) | collective-permute-done | bytes 131104 | tf_op jit(solution)/shard_map/ppermute | solution.py:133
  67.8 1.9 %collective-permute-start.2 = (f32[128,256]{1,0:T(8,128)S(1)}, f32[128,256]{1,0:T(8,128)S(1)}, u32[]{:S(2)}, u32[]{:S(2)}) collective-permute-start(f32[128,256]{1,0:T(8,128)S(1)} %collective-permute-done.refs_1_), channel_id=1, source_target_pairs={{0,64},{32,96},{64,128},{96,160},{128,192},{160,224},{192,256},{22... | collective-permute-start | bytes 393224 | tf_op jit(solution)/shard_map/ppermute | solution.py:133
  69.7 0.0 collective-permute-done.1.refs_2_
  69.7 5.5 %collective-permute-start.3 = (f32[128,256]{1,0:T(8,128)S(1)}, f32[128,256]{1,0:T(8,128)S(1)}, u32[]{:S(2)}, u32[]{:S(2)}) collective-permute-start(f32[128,256]{1,0:T(8,128)S(1)} %collective-permute-done.1.refs_2_), channel_id=1, source_target_pairs={{0,448},{32,480},{64,0},{96,32},{128,64},{160,96},{192,128},{224,1... | collective-permute-start | bytes 393224 | tf_op jit(solution)/shard_map/ppermute | solution.py:134
  75.2 1.1 collective-permute-done.2.refs_3_
  76.3 2.8 %collective-permute-start.4 = (f32[128,256]{1,0:T(8,128)S(1)}, f32[128,256]{1,0:T(8,128)S(1)}, u32[]{:S(2)}, u32[]{:S(2)}) collective-permute-start(f32[128,256]{1,0:T(8,128)S(1)} %collective-permute-done.2.refs_3_), channel_id=1, source_target_pairs={{0,64},{32,96},{64,128},{96,160},{128,192},{160,224},{192,256},{22... | collective-permute-start | bytes 393224 | tf_op jit(solution)/shard_map/ppermute | solution.py:133
  79.2 0.0 collective-permute-done.3.refs_4_
  79.2 4.5 %collective-permute-start.5 = (f32[128,256]{1,0:T(8,128)S(1)}, f32[128,256]{1,0:T(8,128)S(1)}, u32[]{:S(2)}, u32[]{:S(2)}) collective-permute-start(f32[128,256]{1,0:T(8,128)S(1)} %collective-permute-done.3.refs_4_), channel_id=1, source_target_pairs={{0,448},{32,480},{64,0},{96,32},{128,64},{160,96},{192,128},{224,1... | collective-permute-start | bytes 393224 | tf_op jit(solution)/shard_map/ppermute | solution.py:134
  83.7 0.5 collective-permute-done.4.refs_5_
  84.2 4.5 %collective-permute-start.6 = (f32[128,256]{1,0:T(8,128)S(1)}, f32[128,256]{1,0:T(8,128)S(1)}, u32[]{:S(2)}, u32[]{:S(2)}) collective-permute-start(f32[128,256]{1,0:T(8,128)S(1)} %collective-permute-done.4.refs_5_), channel_id=1, source_target_pairs={{0,64},{32,96},{64,128},{96,160},{128,192},{160,224},{192,256},{22... | collective-permute-start | bytes 393224 | tf_op jit(solution)/shard_map/ppermute | solution.py:136
  88.8 1.3 collective-permute-done.5.refs_6_
  90.0 3.0 %collective-permute-done.6.refs_7_ = f32[128,256]{1,0:T(8,128)S(1)} collective-permute-done((f32[128,256]{1,0:T(8,128)S(1)}, f32[128,256]{1,0:T(8,128)S(1)}, u32[]{:S(2)}, u32[]{:S(2)}) %collective-permute-start.6) | collective-permute-done | bytes 131104 | tf_op jit(solution)/shard_map/ppermute | solution.py:136
  93.0 0.0 collective-permute-done.8.refs_9_
  93.0 1.2 shard_map.29
  94.3 4.6 %collective-permute-start.9 = (f32[128,256]{1,0:T(8,128)S(1)}, f32[128,256]{1,0:T(8,128)S(1)}, u32[]{:S(2)}, u32[]{:S(2)}) collective-permute-start(f32[128,256]{1,0:T(8,128)S(1)} %get-tuple-element.9), channel_id=1, source_target_pairs={{0,32},{32,0},{64,96},{96,64},{128,160},{160,128},{192,224},{224,1... | collective-permute-start | bytes 393224 | tf_op jit(solution)/shard_map/ppermute | solution.py:166
  98.9 2.3 %collective-permute-done.9 = f32[128,256]{1,0:T(8,128)S(1)} collective-permute-done((f32[128,256]{1,0:T(8,128)S(1)}, f32[128,256]{1,0:T(8,128)S(1)}, u32[]{:S(2)}, u32[]{:S(2)}) %collective-permute-start.9) | collective-permute-done | bytes 131104 | tf_op jit(solution)/shard_map/ppermute | solution.py:166
  101.2 0.2 broadcast_in_dim.5
  101.5 27.3 %all_to_all.11.mine_ref = f32[16,128,256]{2,1,0:T(8,128)S(1)} all-to-all(f32[16,128,256]{2,1,0:T(8,128)S(1)} %broadcast_in_dim.5), channel_id=1, replica_groups=mesh['z'=16,'x'=4,'c'=2,'y'=4] {'x','y'}, dimensions={0} | all-to-all | bytes 4194304 | tf_op jit(solution)/shard_map/all_to_all | solution.py:145
  128.7 6.7 %collective-permute-start.11 = (f32[16,128,256]{2,1,0:T(8,128)S(1)}, f32[16,128,256]{2,1,0:T(8,128)S(1)}, u32[]{:S(2)}, u32[]{:S(2)}) collective-permute-start(f32[16,128,256]{2,1,0:T(8,128)S(1)} %all_to_all.11.mine_ref), channel_id=1, source_target_pairs={{0,4},{4,0},{1,5},{5,1},{2,6},{6,2},{3,7},{7,3},{8,12},{12,8},{9,1... | collective-permute-start | bytes 6291464 | tf_op jit(solution)/shard_map/ppermute | solution.py:169
  135.5 3.5 %collective-permute-start.10 = (f32[8,128,256]{2,1,0:T(8,128)S(1)}, f32[8,128,256]{2,1,0:T(8,128)S(1)}, u32[]{:S(2)}, u32[]{:S(2)}) collective-permute-start(f32[8,128,256]{2,1,0:T(8,128)S(1)} %get-tuple-element.10.here_ref), channel_id=1, source_target_pairs={{0,32},{32,0},{64,96},{96,64},{128,160},{160,128},{192,224},{224,1... | collective-permute-start | bytes 3145736 | tf_op jit(solution)/shard_map/ppermute | solution.py:167
  139.0 23.4 %collective-permute-done.10.there_ref = f32[8,128,256]{2,1,0:T(8,128)S(1)} collective-permute-done((f32[8,128,256]{2,1,0:T(8,128)S(1)}, f32[8,128,256]{2,1,0:T(8,128)S(1)}, u32[]{:S(2)}, u32[]{:S(2)}) %collective-permute-start.10) | collective-permute-done | bytes 1048608 | tf_op jit(solution)/shard_map/ppermute | solution.py:167
  162.4 0.0 collective-permute-done.11.other_ref
  162.4 1.7 %shard_map.30 = f32[128,256]{1,0:T(8,128)} custom-call(f32[128,256]{1,0:T(8,128)S(1)} %add.3.square_ref, f32[8,128,256]{2,1,0:T(8,128)S(1)} %get-tuple-element.10.here_ref, f32[8,128,256]{2,1,0:T(8,128)S(1)} %collective-permute-done.10.there_ref, f32[16,128,256]{2,1,0:T(8,128)S(1)} %all_to_all.11.mine_ref, f32[16,128,256]{2,1,0:T(8,128)S(1)} %collective-permute-done.11.other_ref), custom_call_target="tpu_custom_call" | custom-call | flops 805306368 | bytes 6291456 | tf_op jit(solution)/shard_map/pallas_call | solution.py:115
  (1 shorter events, 0.0 us)
Async XLA Ops:
  1.6 0.7 collective-permute-start.7
  3.5 46.0 %copy-start = (f32[128,256]{1,0:T(8,128)S(1)}, f32[128,256]{1,0:T(8,128)}, u32[]{:S(2)}) copy-start(f32[128,256]{1,0:T(8,128)} %shard_map.28.refs_0_) | copy-start | bytes 393220
  44.3 48.7 %collective-permute-start.8 = (f32[16,128,256]{2,1,0:T(8,128)S(1)}, f32[16,128,256]{2,1,0:T(8,128)S(1)}, u32[]{:S(2)}, u32[]{:S(2)}) collective-permute-start(f32[16,128,256]{2,1,0:T(8,128)S(1)} %all_to_all.10.refs_8_), channel_id=1, source_target_pairs={{0,4},{4,0},{1,5},{5,1},{2,6},{6,2},{3,7},{7,3},{8,12},{12,8},{9,1... | collective-permute-start | bytes 6291464 | tf_op jit(solution)/shard_map/ppermute | solution.py:164
  49.5 18.3 %collective-permute-start = (f32[128,256]{1,0:T(8,128)S(1)}, f32[128,256]{1,0:T(8,128)S(1)}, u32[]{:S(2)}, u32[]{:S(2)}) collective-permute-start(f32[128,256]{1,0:T(8,128)S(1)} %copy-done), channel_id=1, source_target_pairs={{0,64},{32,96},{64,128},{96,160},{128,192},{160,224},{192,256},{22... | collective-permute-start | bytes 393224 | tf_op jit(solution)/shard_map/ppermute | solution.py:133
  54.4 15.3 %collective-permute-start.1 = (f32[128,256]{1,0:T(8,128)S(1)}, f32[128,256]{1,0:T(8,128)S(1)}, u32[]{:S(2)}, u32[]{:S(2)}) collective-permute-start(f32[128,256]{1,0:T(8,128)S(1)} %copy-done), channel_id=1, source_target_pairs={{0,448},{32,480},{64,0},{96,32},{128,64},{160,96},{192,128},{224,1... | collective-permute-start | bytes 393224 | tf_op jit(solution)/shard_map/ppermute | solution.py:134
  67.8 8.5 %collective-permute-start.2 = (f32[128,256]{1,0:T(8,128)S(1)}, f32[128,256]{1,0:T(8,128)S(1)}, u32[]{:S(2)}, u32[]{:S(2)}) collective-permute-start(f32[128,256]{1,0:T(8,128)S(1)} %collective-permute-done.refs_1_), channel_id=1, source_target_pairs={{0,64},{32,96},{64,128},{96,160},{128,192},{160,224},{192,256},{22... | collective-permute-start | bytes 393224 | tf_op jit(solution)/shard_map/ppermute | solution.py:133
  69.7 9.5 %collective-permute-start.3 = (f32[128,256]{1,0:T(8,128)S(1)}, f32[128,256]{1,0:T(8,128)S(1)}, u32[]{:S(2)}, u32[]{:S(2)}) collective-permute-start(f32[128,256]{1,0:T(8,128)S(1)} %collective-permute-done.1.refs_2_), channel_id=1, source_target_pairs={{0,448},{32,480},{64,0},{96,32},{128,64},{160,96},{192,128},{224,1... | collective-permute-start | bytes 393224 | tf_op jit(solution)/shard_map/ppermute | solution.py:134
  76.3 7.9 %collective-permute-start.4 = (f32[128,256]{1,0:T(8,128)S(1)}, f32[128,256]{1,0:T(8,128)S(1)}, u32[]{:S(2)}, u32[]{:S(2)}) collective-permute-start(f32[128,256]{1,0:T(8,128)S(1)} %collective-permute-done.2.refs_3_), channel_id=1, source_target_pairs={{0,64},{32,96},{64,128},{96,160},{128,192},{160,224},{192,256},{22... | collective-permute-start | bytes 393224 | tf_op jit(solution)/shard_map/ppermute | solution.py:133
  79.2 10.9 %collective-permute-start.5 = (f32[128,256]{1,0:T(8,128)S(1)}, f32[128,256]{1,0:T(8,128)S(1)}, u32[]{:S(2)}, u32[]{:S(2)}) collective-permute-start(f32[128,256]{1,0:T(8,128)S(1)} %collective-permute-done.3.refs_4_), channel_id=1, source_target_pairs={{0,448},{32,480},{64,0},{96,32},{128,64},{160,96},{192,128},{224,1... | collective-permute-start | bytes 393224 | tf_op jit(solution)/shard_map/ppermute | solution.py:134
  84.2 8.8 %collective-permute-start.6 = (f32[128,256]{1,0:T(8,128)S(1)}, f32[128,256]{1,0:T(8,128)S(1)}, u32[]{:S(2)}, u32[]{:S(2)}) collective-permute-start(f32[128,256]{1,0:T(8,128)S(1)} %collective-permute-done.4.refs_5_), channel_id=1, source_target_pairs={{0,64},{32,96},{64,128},{96,160},{128,192},{160,224},{192,256},{22... | collective-permute-start | bytes 393224 | tf_op jit(solution)/shard_map/ppermute | solution.py:136
  94.3 7.0 %collective-permute-start.9 = (f32[128,256]{1,0:T(8,128)S(1)}, f32[128,256]{1,0:T(8,128)S(1)}, u32[]{:S(2)}, u32[]{:S(2)}) collective-permute-start(f32[128,256]{1,0:T(8,128)S(1)} %get-tuple-element.9), channel_id=1, source_target_pairs={{0,32},{32,0},{64,96},{96,64},{128,160},{160,128},{192,224},{224,1... | collective-permute-start | bytes 393224 | tf_op jit(solution)/shard_map/ppermute | solution.py:166
  128.7 33.7 %collective-permute-start.11 = (f32[16,128,256]{2,1,0:T(8,128)S(1)}, f32[16,128,256]{2,1,0:T(8,128)S(1)}, u32[]{:S(2)}, u32[]{:S(2)}) collective-permute-start(f32[16,128,256]{2,1,0:T(8,128)S(1)} %all_to_all.11.mine_ref), channel_id=1, source_target_pairs={{0,4},{4,0},{1,5},{5,1},{2,6},{6,2},{3,7},{7,3},{8,12},{12,8},{9,1... | collective-permute-start | bytes 6291464 | tf_op jit(solution)/shard_map/ppermute | solution.py:169
  135.5 26.9 %collective-permute-start.10 = (f32[8,128,256]{2,1,0:T(8,128)S(1)}, f32[8,128,256]{2,1,0:T(8,128)S(1)}, u32[]{:S(2)}, u32[]{:S(2)}) collective-permute-start(f32[8,128,256]{2,1,0:T(8,128)S(1)} %get-tuple-element.10.here_ref), channel_id=1, source_target_pairs={{0,32},{32,0},{64,96},{96,64},{128,160},{160,128},{192,224},{224,1... | collective-permute-start | bytes 3145736 | tf_op jit(solution)/shard_map/ppermute | solution.py:167

commit v3 on v1

v3 whole, which is shorter than its diff:
```python
import functools

import jax
import jax.numpy as jnp
from jax import lax
from jax.experimental import pallas as pl
from jax.experimental.pallas import tpu as pltpu
from jax.sharding import Mesh
from jax.sharding import PartitionSpec as P


TILE = 128
LAYERS = 16
HALF = 8
DISTANCES = (0, -1, 1, -2, 2, -3, 3, -4)


VMEM = pl.BlockSpec(memory_space=pltpu.VMEM)


def shape(*dims):
    return jax.ShapeDtypeStruct(dims, jnp.float32)


def split(value):
    high = value.astype(jnp.bfloat16)
    low = (value - high.astype(jnp.float32)).astype(jnp.bfloat16)
    return high, low


def stack(left):
    high, low = split(left)
    return jnp.concatenate([high, low], 0)


def times(left, right):
    high, low = split(right)
    both = jnp.dot(left, high, preferred_element_type=jnp.float32)
    cross = jnp.dot(left[:TILE], low, preferred_element_type=jnp.float32)
    return both[:TILE] + (both[TILE:] + cross)


def kept(rows_ref, row, layer):
    return rows_ref[pl.ds(row, 1), pl.ds(pl.multiple_of(256 * layer, 256), 256)]


def place():
    layer = lax.axis_index("z")
    return layer, lax.div(layer, 2), lax.rem(layer, 2)


def masked_pair(block_ref, rows_ref, x, half, slot, layer):
    parity = lax.rem(lax.axis_index("z"), 2)
    first = 8 * x + 4 * half + 2 * parity
    return jnp.concatenate(
        [block_ref[4 * x + slot + i] * kept(rows_ref, first + i, layer) for i in range(2)], 0
    )


def near_kernel(*refs):
    lefts = refs[:HALF]
    mine_ref, rows_ref, own_ref, away_ref, panel_ref = refs[HALF:]
    layer, pair, parity = place()
    core = lax.axis_index("c")
    row = 8 * lax.axis_index("x") + 4 * core + lax.axis_index("y")
    for distance, left_ref in zip(DISTANCES, lefts, strict=True):
        slot = lax.rem(pair + (distance + HALF), HALF)
        panel_ref[slot] = left_ref[...] * kept(rows_ref, row, 2 * slot + parity)
    own = away = jnp.zeros((TILE, 2 * TILE), jnp.float32)
    for x in range(4):
        left = stack(panel_ref[2 * x + core])
        own += times(left, masked_pair(mine_ref, rows_ref, x, core, 2 * parity, layer))
        away += times(
            left,
            masked_pair(mine_ref, rows_ref, x, core, 2 - 2 * parity, layer + 1 - 2 * parity),
        )
    own_ref[...] = own
    away_ref[...] = away


def far_kernel(away, panel_ref, other_ref, rows_ref, start_ref, out_ref):
    layer, _, parity = place()
    half = 1 - lax.axis_index("c")
    total = start_ref[...]
    slot = 2 - 2 * parity if away else 2 * parity
    slab = layer + 1 - 2 * parity if away else layer
    for x in range(4):
        right = masked_pair(other_ref, rows_ref, x, half, slot, slab)
        total += times(stack(panel_ref[2 * x + half]), right)
    out_ref[...] = total


def cube_half(here_ref, there_ref, block_ref, half):
    parity = lax.rem(lax.axis_index("z"), 2)
    total = jnp.zeros((TILE, 2 * TILE), jnp.float32)
    for x in range(4):
        for panel_ref, which in ((here_ref, parity), (there_ref, 1 - parity)):
            right = block_ref[pl.ds(4 * x + 2 * which, 2)].reshape(2 * TILE, 2 * TILE)
            total += times(stack(panel_ref[2 * x + half]), right)
    return total


def cube_near_kernel(square_ref, here_ref, there_ref, mine_ref, out_ref):
    cube = cube_half(here_ref, there_ref, mine_ref, lax.axis_index("c"))
    out_ref[...] = 3.0 * square_ref[...] - 2.0 * cube


def cube_far_kernel(start_ref, here_ref, there_ref, other_ref, out_ref):
    cube = cube_half(here_ref, there_ref, other_ref, 1 - lax.axis_index("c"))
    out_ref[...] = start_ref[...] - 2.0 * cube


def call(kernel, out_shape, *operands):
    return pl.pallas_call(
        kernel,
        out_shape=out_shape,
        in_specs=[VMEM] * len(operands),
        out_specs=jax.tree.map(lambda _: VMEM, out_shape),
        compiler_params=pltpu.CompilerParams(vmem_limit_bytes=12 << 20),
        cost_estimate=pl.CostEstimate(
            flops=3 * 128 * 2048 * 512, bytes_accessed=3 << 20, transcendentals=0
        ),
    )(*operands)


def ring(block):
    up = [(z, (z + 2) % LAYERS) for z in range(LAYERS)]
    down = [(z, (z - 2) % LAYERS) for z in range(LAYERS)]
    blocks = [block]
    ahead = behind = block
    for _ in range(1, 4):
        ahead = lax.ppermute(ahead, "z", up)
        behind = lax.ppermute(behind, "z", down)
        blocks += [ahead, behind]
    blocks.append(lax.ppermute(ahead, "z", up))
    return blocks


def spread(block):
    return jnp.broadcast_to(block[None], (16, *block.shape))


def to_plane(copies):
    return lax.all_to_all(copies, ("x", "y"), 0, 0)


CORES = [(0, 1), (1, 0)]
NEIGHBOURS = [(z, z ^ 1) for z in range(LAYERS)]
SWAP = [
    (4 * z + y, 4 * (z ^ 1) + (y ^ 2))
    for z in range(LAYERS)
    for y in range(4)
    if z % 2 != y // 2
]


def on_device(density, pattern):
    block = shape(TILE, 2 * TILE)
    matched = lax.rem(lax.axis_index("z"), 2) == lax.div(lax.axis_index("y"), 2)
    rows = jnp.repeat(pattern.astype(jnp.float32), TILE, axis=1)
    moved = lax.ppermute(density, ("z", "y"), SWAP)
    lefts = ring(density)
    mine = to_plane(spread(jnp.where(matched, density, moved)))
    other = lax.ppermute(mine, "c", CORES)
    own, away, here = call(
        near_kernel, (block, block, shape(HALF, TILE, 2 * TILE)), *lefts, mine, rows
    )
    away = call(functools.partial(far_kernel, True), block, here, other, rows, away)
    own = call(functools.partial(far_kernel, False), block, here, other, rows, own)
    square = own + lax.ppermute(away, "z", NEIGHBOURS)
    there = lax.ppermute(here, "z", NEIGHBOURS)
    mine = to_plane(spread(square))
    other = lax.ppermute(mine, "c", CORES)
    start = call(cube_near_kernel, block, square, here, there, mine)
    return call(cube_far_kernel, block, start, here, there, other)


def solution(mesh):
    split_mesh = Mesh(mesh.devices.reshape(LAYERS, 4, 2, 4), ("z", "x", "c", "y"))
    return jax.shard_map(
        on_device,
        mesh=split_mesh,
        in_specs=(P(("x", "c", "y"), "z"), P()),
        out_specs=P(("x", "c", "y"), "z"),
        check_vma=False,
    )
```

time: 165 us -> 163 us (0.988)
    pallas_call x3 -> x5, Pallas kernels: 3.82 us -> 3.46 us  [call(): pl.pallas_call(kernel, out_shape=out_shape, in_specs=[VMEM] * len(operand...]
  transfers between devices with their start and end apart: 12 -> 12, of which waited for: 7 -> 7; matrix products, arithmetic and copies ran while one was open for 0% -> 0% of each run, Pallas kernels for 0% -> 1%
where the time goes in v3:
time: 163 us
  blocking collectives  68.1 us (42%)
  starting transfers between devices  53.4 us (33%)
  waiting for transfers between devices  35.5 us (22%)
  Pallas kernels  3.46 us (2%)
    all_to_all x2, blocking collectives, to_plane(): return lax.all_to_all(copies, ('x', 'y'), 0, 0)  68.1 us
    ppermute x1, waiting for transfers between devices, on_device(): there = lax.ppermute(here, 'z', NEIGHBOURS)  23.4 us
    ppermute x3, starting transfers between devices, ring(): behind = lax.ppermute(behind, 'z', down)  18.6 us
    ppermute x2, starting transfers between devices, on_device(): other = lax.ppermute(mine, 'c', CORES)  11.8 us
    ppermute x3, starting transfers between devices, ring(): ahead = lax.ppermute(ahead, 'z', up)  9.65 us
    ppermute x3, waiting for transfers between devices, ring(): ahead = lax.ppermute(ahead, 'z', up)  6.45 us
    ppermute x1, starting transfers between devices, on_device(): square = own + lax.ppermute(away, 'z', NEIGHBOURS)  4.63 us
    ppermute x1, starting transfers between devices, ring(): blocks.append(lax.ppermute(ahead, 'z', up))  4.51 us
  transfers between devices with their start and end apart: 12, of which 7 were waited for; matrix products, arithmetic and copies ran while one was open for 0% of the time, Pallas kernels for 1%

profile of v3, /device:TPU:1, one launch (start us, length us, event | category | flops | bytes accessed | tf_op | source)
XLA Modules:
  0.0 162.6 jit_solution(9754232384526324577)
XLA Ops:
  0.0 0.7 collective-permute-start.7
  0.7 0.0 collective-permute-done.7
  0.7 0.9 broadcast_select_fusion
  1.6 0.2 broadcast_in_dim.6
  1.8 0.0 copy-start
  1.8 0.0 copy-start.1
  1.8 40.9 %all_to_all.10.refs_8_ = f32[16,128,256]{2,1,0:T(8,128)S(1)} all-to-all(f32[16,128,256]{2,1,0:T(8,128)S(1)} %broadcast_in_dim.6), channel_id=1, replica_groups=mesh['z'=16,'x'=4,'c'=2,'y'=4] {'x','y'}, dimensions={0} | all-to-all | bytes 4194304 | tf_op jit(solution)/shard_map/all_to_all | solution.py:144
  42.7 5.1 %collective-permute-start.8 = (f32[16,128,256]{2,1,0:T(8,128)S(1)}, f32[16,128,256]{2,1,0:T(8,128)S(1)}, u32[]{:S(2)}, u32[]{:S(2)}) collective-permute-start(f32[16,128,256]{2,1,0:T(8,128)S(1)} %all_to_all.10.refs_8_), channel_id=1, source_target_pairs={{0,4},{4,0},{1,5},{5,1},{2,6},{6,2},{3,7},{7,3},{8,12},{12,8},{9,1... | collective-permute-start | bytes 6291464 | tf_op jit(solution)/shard_map/ppermute | solution.py:164
  47.8 0.0 copy-done
  47.9 4.9 %collective-permute-start = (f32[128,256]{1,0:T(8,128)S(1)}, f32[128,256]{1,0:T(8,128)S(1)}, u32[]{:S(2)}, u32[]{:S(2)}) collective-permute-start(f32[128,256]{1,0:T(8,128)S(1)} %copy-done), channel_id=1, source_target_pairs={{0,64},{32,96},{64,128},{96,160},{128,192},{160,224},{192,256},{22... | collective-permute-start | bytes 393224 | tf_op jit(solution)/shard_map/ppermute | solution.py:132
  52.8 8.6 %collective-permute-start.1 = (f32[128,256]{1,0:T(8,128)S(1)}, f32[128,256]{1,0:T(8,128)S(1)}, u32[]{:S(2)}, u32[]{:S(2)}) collective-permute-start(f32[128,256]{1,0:T(8,128)S(1)} %copy-done), channel_id=1, source_target_pairs={{0,448},{32,480},{64,0},{96,32},{128,64},{160,96},{192,128},{224,1... | collective-permute-start | bytes 393224 | tf_op jit(solution)/shard_map/ppermute | solution.py:133
  61.4 4.8 %collective-permute-done.refs_1_ = f32[128,256]{1,0:T(8,128)S(1)} collective-permute-done((f32[128,256]{1,0:T(8,128)S(1)}, f32[128,256]{1,0:T(8,128)S(1)}, u32[]{:S(2)}, u32[]{:S(2)}) %collective-permute-start) | collective-permute-done | bytes 131104 | tf_op jit(solution)/shard_map/ppermute | solution.py:132
  66.2 1.9 %collective-permute-start.2 = (f32[128,256]{1,0:T(8,128)S(1)}, f32[128,256]{1,0:T(8,128)S(1)}, u32[]{:S(2)}, u32[]{:S(2)}) collective-permute-start(f32[128,256]{1,0:T(8,128)S(1)} %collective-permute-done.refs_1_), channel_id=1, source_target_pairs={{0,64},{32,96},{64,128},{96,160},{128,192},{160,224},{192,256},{22... | collective-permute-start | bytes 393224 | tf_op jit(solution)/shard_map/ppermute | solution.py:132
  68.1 0.0 collective-permute-done.1.refs_2_
  68.1 5.5 %collective-permute-start.3 = (f32[128,256]{1,0:T(8,128)S(1)}, f32[128,256]{1,0:T(8,128)S(1)}, u32[]{:S(2)}, u32[]{:S(2)}) collective-permute-start(f32[128,256]{1,0:T(8,128)S(1)} %collective-permute-done.1.refs_2_), channel_id=1, source_target_pairs={{0,448},{32,480},{64,0},{96,32},{128,64},{160,96},{192,128},{224,1... | collective-permute-start | bytes 393224 | tf_op jit(solution)/shard_map/ppermute | solution.py:133
  73.6 1.1 collective-permute-done.2.refs_3_
  74.7 2.8 %collective-permute-start.4 = (f32[128,256]{1,0:T(8,128)S(1)}, f32[128,256]{1,0:T(8,128)S(1)}, u32[]{:S(2)}, u32[]{:S(2)}) collective-permute-start(f32[128,256]{1,0:T(8,128)S(1)} %collective-permute-done.2.refs_3_), channel_id=1, source_target_pairs={{0,64},{32,96},{64,128},{96,160},{128,192},{160,224},{192,256},{22... | collective-permute-start | bytes 393224 | tf_op jit(solution)/shard_map/ppermute | solution.py:132
  77.6 0.0 collective-permute-done.3.refs_4_
  77.6 4.5 %collective-permute-start.5 = (f32[128,256]{1,0:T(8,128)S(1)}, f32[128,256]{1,0:T(8,128)S(1)}, u32[]{:S(2)}, u32[]{:S(2)}) collective-permute-start(f32[128,256]{1,0:T(8,128)S(1)} %collective-permute-done.3.refs_4_), channel_id=1, source_target_pairs={{0,448},{32,480},{64,0},{96,32},{128,64},{160,96},{192,128},{224,1... | collective-permute-start | bytes 393224 | tf_op jit(solution)/shard_map/ppermute | solution.py:133
  82.1 0.5 collective-permute-done.4.refs_5_
  82.6 4.5 %collective-permute-start.6 = (f32[128,256]{1,0:T(8,128)S(1)}, f32[128,256]{1,0:T(8,128)S(1)}, u32[]{:S(2)}, u32[]{:S(2)}) collective-permute-start(f32[128,256]{1,0:T(8,128)S(1)} %collective-permute-done.4.refs_5_), channel_id=1, source_target_pairs={{0,64},{32,96},{64,128},{96,160},{128,192},{160,224},{192,256},{22... | collective-permute-start | bytes 393224 | tf_op jit(solution)/shard_map/ppermute | solution.py:135
  87.1 0.0 copy-done.1
  87.2 0.2 broadcast_in_dim.7
  87.4 0.3 copy.5
  87.7 0.8 collective-permute-done.5.refs_6_
  88.4 3.0 %collective-permute-done.6.refs_7_ = f32[128,256]{1,0:T(8,128)S(1)} collective-permute-done((f32[128,256]{1,0:T(8,128)S(1)}, f32[128,256]{1,0:T(8,128)S(1)}, u32[]{:S(2)}, u32[]{:S(2)}) %collective-permute-start.6) | collective-permute-done | bytes 131104 | tf_op jit(solution)/shard_map/ppermute | solution.py:135
  91.4 0.8 shard_map.28
  92.2 0.0 collective-permute-done.8.other_ref
  92.2 0.4 shard_map.30
  92.6 4.6 %collective-permute-start.9 = (f32[128,256]{1,0:T(8,128)S(1)}, f32[128,256]{1,0:T(8,128)S(1)}, u32[]{:S(2)}, u32[]{:S(2)}) collective-permute-start(f32[128,256]{1,0:T(8,128)S(1)} %shard_map.30), channel_id=1, source_target_pairs={{0,32},{32,0},{64,96},{96,64},{128,160},{160,128},{192,224},{224,1... | collective-permute-start | bytes 393224 | tf_op jit(solution)/shard_map/ppermute | solution.py:170
  97.2 0.4 shard_map.29
  97.6 1.9 %collective-permute-done.9 = f32[128,256]{1,0:T(8,128)S(1)} collective-permute-done((f32[128,256]{1,0:T(8,128)S(1)}, f32[128,256]{1,0:T(8,128)S(1)}, u32[]{:S(2)}, u32[]{:S(2)}) %collective-permute-start.9) | collective-permute-done | bytes 131104 | tf_op jit(solution)/shard_map/ppermute | solution.py:170
  99.6 0.2 broadcast_in_dim.8
  99.8 27.3 %all_to_all.11.mine_ref = f32[16,128,256]{2,1,0:T(8,128)S(1)} all-to-all(f32[16,128,256]{2,1,0:T(8,128)S(1)} %broadcast_in_dim.8), channel_id=1, replica_groups=mesh['z'=16,'x'=4,'c'=2,'y'=4] {'x','y'}, dimensions={0} | all-to-all | bytes 4194304 | tf_op jit(solution)/shard_map/all_to_all | solution.py:144
  127.1 6.7 %collective-permute-start.11 = (f32[16,128,256]{2,1,0:T(8,128)S(1)}, f32[16,128,256]{2,1,0:T(8,128)S(1)}, u32[]{:S(2)}, u32[]{:S(2)}) collective-permute-start(f32[16,128,256]{2,1,0:T(8,128)S(1)} %all_to_all.11.mine_ref), channel_id=1, source_target_pairs={{0,4},{4,0},{1,5},{5,1},{2,6},{6,2},{3,7},{7,3},{8,12},{12,8},{9,1... | collective-permute-start | bytes 6291464 | tf_op jit(solution)/shard_map/ppermute | solution.py:173
  133.8 3.5 %collective-permute-start.10 = (f32[8,128,256]{2,1,0:T(8,128)S(1)}, f32[8,128,256]{2,1,0:T(8,128)S(1)}, u32[]{:S(2)}, u32[]{:S(2)}) collective-permute-start(f32[8,128,256]{2,1,0:T(8,128)S(1)} %get-tuple-element.8.panel_ref.here_ref), channel_id=1, source_target_pairs={{0,32},{32,0},{64,96},{96,64},{128,160},{160,128},{192,224},{224,1... | collective-permute-start | bytes 3145736 | tf_op jit(solution)/shard_map/ppermute | solution.py:171
  137.3 23.4 %collective-permute-done.10.there_ref = f32[8,128,256]{2,1,0:T(8,128)S(1)} collective-permute-done((f32[8,128,256]{2,1,0:T(8,128)S(1)}, f32[8,128,256]{2,1,0:T(8,128)S(1)}, u32[]{:S(2)}, u32[]{:S(2)}) %collective-permute-start.10) | collective-permute-done | bytes 1048608 | tf_op jit(solution)/shard_map/ppermute | solution.py:171
  160.7 0.6 shard_map.31.start_ref
  161.3 0.0 collective-permute-done.11.other_ref
  161.3 1.3 shard_map.32
  (2 shorter events, 0.0 us)
Async XLA Ops:
  0.0 0.7 collective-permute-start.7
  1.8 46.0 %copy-start = (f32[128,256]{1,0:T(8,128)S(1)}, f32[128,256]{1,0:T(8,128)}, u32[]{:S(2)}) copy-start(f32[128,256]{1,0:T(8,128)} %refs_0_.1) | copy-start | bytes 393220
  1.8 85.3 %copy-start.1 = (s32[32,32]{1,0:T(8,128)S(1)}, s32[32,32]{1,0:T(8,128)}, u32[]{:S(2)}) copy-start(s32[32,32]{1,0:T(8,128)} %param.3) | copy-start | bytes 12292
  42.7 49.4 %collective-permute-start.8 = (f32[16,128,256]{2,1,0:T(8,128)S(1)}, f32[16,128,256]{2,1,0:T(8,128)S(1)}, u32[]{:S(2)}, u32[]{:S(2)}) collective-permute-start(f32[16,128,256]{2,1,0:T(8,128)S(1)} %all_to_all.10.refs_8_), channel_id=1, source_target_pairs={{0,4},{4,0},{1,5},{5,1},{2,6},{6,2},{3,7},{7,3},{8,12},{12,8},{9,1... | collective-permute-start | bytes 6291464 | tf_op jit(solution)/shard_map/ppermute | solution.py:164
  47.9 18.3 %collective-permute-start = (f32[128,256]{1,0:T(8,128)S(1)}, f32[128,256]{1,0:T(8,128)S(1)}, u32[]{:S(2)}, u32[]{:S(2)}) collective-permute-start(f32[128,256]{1,0:T(8,128)S(1)} %copy-done), channel_id=1, source_target_pairs={{0,64},{32,96},{64,128},{96,160},{128,192},{160,224},{192,256},{22... | collective-permute-start | bytes 393224 | tf_op jit(solution)/shard_map/ppermute | solution.py:132
  52.8 15.3 %collective-permute-start.1 = (f32[128,256]{1,0:T(8,128)S(1)}, f32[128,256]{1,0:T(8,128)S(1)}, u32[]{:S(2)}, u32[]{:S(2)}) collective-permute-start(f32[128,256]{1,0:T(8,128)S(1)} %copy-done), channel_id=1, source_target_pairs={{0,448},{32,480},{64,0},{96,32},{128,64},{160,96},{192,128},{224,1... | collective-permute-start | bytes 393224 | tf_op jit(solution)/shard_map/ppermute | solution.py:133
  66.2 8.5 %collective-permute-start.2 = (f32[128,256]{1,0:T(8,128)S(1)}, f32[128,256]{1,0:T(8,128)S(1)}, u32[]{:S(2)}, u32[]{:S(2)}) collective-permute-start(f32[128,256]{1,0:T(8,128)S(1)} %collective-permute-done.refs_1_), channel_id=1, source_target_pairs={{0,64},{32,96},{64,128},{96,160},{128,192},{160,224},{192,256},{22... | collective-permute-start | bytes 393224 | tf_op jit(solution)/shard_map/ppermute | solution.py:132
  68.1 9.5 %collective-permute-start.3 = (f32[128,256]{1,0:T(8,128)S(1)}, f32[128,256]{1,0:T(8,128)S(1)}, u32[]{:S(2)}, u32[]{:S(2)}) collective-permute-start(f32[128,256]{1,0:T(8,128)S(1)} %collective-permute-done.1.refs_2_), channel_id=1, source_target_pairs={{0,448},{32,480},{64,0},{96,32},{128,64},{160,96},{192,128},{224,1... | collective-permute-start | bytes 393224 | tf_op jit(solution)/shard_map/ppermute | solution.py:133
  74.7 7.9 %collective-permute-start.4 = (f32[128,256]{1,0:T(8,128)S(1)}, f32[128,256]{1,0:T(8,128)S(1)}, u32[]{:S(2)}, u32[]{:S(2)}) collective-permute-start(f32[128,256]{1,0:T(8,128)S(1)} %collective-permute-done.2.refs_3_), channel_id=1, source_target_pairs={{0,64},{32,96},{64,128},{96,160},{128,192},{160,224},{192,256},{22... | collective-permute-start | bytes 393224 | tf_op jit(solution)/shard_map/ppermute | solution.py:132
  77.6 10.9 %collective-permute-start.5 = (f32[128,256]{1,0:T(8,128)S(1)}, f32[128,256]{1,0:T(8,128)S(1)}, u32[]{:S(2)}, u32[]{:S(2)}) collective-permute-start(f32[128,256]{1,0:T(8,128)S(1)} %collective-permute-done.3.refs_4_), channel_id=1, source_target_pairs={{0,448},{32,480},{64,0},{96,32},{128,64},{160,96},{192,128},{224,1... | collective-permute-start | bytes 393224 | tf_op jit(solution)/shard_map/ppermute | solution.py:133
  82.6 8.8 %collective-permute-start.6 = (f32[128,256]{1,0:T(8,128)S(1)}, f32[128,256]{1,0:T(8,128)S(1)}, u32[]{:S(2)}, u32[]{:S(2)}) collective-permute-start(f32[128,256]{1,0:T(8,128)S(1)} %collective-permute-done.4.refs_5_), channel_id=1, source_target_pairs={{0,64},{32,96},{64,128},{96,160},{128,192},{160,224},{192,256},{22... | collective-permute-start | bytes 393224 | tf_op jit(solution)/shard_map/ppermute | solution.py:135
  92.6 7.0 %collective-permute-start.9 = (f32[128,256]{1,0:T(8,128)S(1)}, f32[128,256]{1,0:T(8,128)S(1)}, u32[]{:S(2)}, u32[]{:S(2)}) collective-permute-start(f32[128,256]{1,0:T(8,128)S(1)} %shard_map.30), channel_id=1, source_target_pairs={{0,32},{32,0},{64,96},{96,64},{128,160},{160,128},{192,224},{224,1... | collective-permute-start | bytes 393224 | tf_op jit(solution)/shard_map/ppermute | solution.py:170
  127.1 34.3 %collective-permute-start.11 = (f32[16,128,256]{2,1,0:T(8,128)S(1)}, f32[16,128,256]{2,1,0:T(8,128)S(1)}, u32[]{:S(2)}, u32[]{:S(2)}) collective-permute-start(f32[16,128,256]{2,1,0:T(8,128)S(1)} %all_to_all.11.mine_ref), channel_id=1, source_target_pairs={{0,4},{4,0},{1,5},{5,1},{2,6},{6,2},{3,7},{7,3},{8,12},{12,8},{9,1... | collective-permute-start | bytes 6291464 | tf_op jit(solution)/shard_map/ppermute | solution.py:173
  133.8 26.9 %collective-permute-start.10 = (f32[8,128,256]{2,1,0:T(8,128)S(1)}, f32[8,128,256]{2,1,0:T(8,128)S(1)}, u32[]{:S(2)}, u32[]{:S(2)}) collective-permute-start(f32[8,128,256]{2,1,0:T(8,128)S(1)} %get-tuple-element.8.panel_ref.here_ref), channel_id=1, source_target_pairs={{0,32},{32,0},{64,96},{96,64},{128,160},{160,128},{192,224},{224,1... | collective-permute-start | bytes 3145736 | tf_op jit(solution)/shard_map/ppermute | solution.py:171

commit v4 on v3

--- a/solution.py
+++ b/solution.py
@@ -147,20 +147,18 @@
 CORES = [(0, 1), (1, 0)]
 NEIGHBOURS = [(z, z ^ 1) for z in range(LAYERS)]
 SWAP = [
-    (4 * z + y, 4 * (z ^ 1) + (y ^ 2))
+    (4 * z + y, 4 * z + y if z % 2 == y // 2 else 4 * (z ^ 1) + (y ^ 2))
     for z in range(LAYERS)
     for y in range(4)
-    if z % 2 != y // 2
 ]
 
 
 def on_device(density, pattern):
     block = shape(TILE, 2 * TILE)
-    matched = lax.rem(lax.axis_index("z"), 2) == lax.div(lax.axis_index("y"), 2)
     rows = jnp.repeat(pattern.astype(jnp.float32), TILE, axis=1)
     moved = lax.ppermute(density, ("z", "y"), SWAP)
     lefts = ring(density)
-    mine = to_plane(spread(jnp.where(matched, density, moved)))
+    mine = to_plane(spread(moved))
     other = lax.ppermute(mine, "c", CORES)
     own, away, here = call(
         near_kernel, (block, block, shape(HALF, TILE, 2 * TILE)), *lefts, mine, rows

time: 163 us -> 163 us (level)
  no operation moved by 1% of the time
where the time goes in v4:
time: 163 us
  blocking collectives  68.2 us (42%)
  starting transfers between devices  54.3 us (33%)
  waiting for transfers between devices  35.5 us (22%)
  Pallas kernels  3.46 us (2%)
    all_to_all x2, blocking collectives, to_plane(): return lax.all_to_all(copies, ('x', 'y'), 0, 0)  68.2 us
    ppermute x1, waiting for transfers between devices, on_device(): there = lax.ppermute(here, 'z', NEIGHBOURS)  23.4 us
    ppermute x3, starting transfers between devices, ring(): behind = lax.ppermute(behind, 'z', down)  18.6 us
    ppermute x2, starting transfers between devices, on_device(): other = lax.ppermute(mine, 'c', CORES)  11.8 us
    ppermute x3, starting transfers between devices, ring(): ahead = lax.ppermute(ahead, 'z', up)  9.65 us
    ppermute x3, waiting for transfers between devices, ring(): ahead = lax.ppermute(ahead, 'z', up)  6.45 us
    ppermute x1, starting transfers between devices, on_device(): square = own + lax.ppermute(away, 'z', NEIGHBOURS)  4.62 us
    ppermute x1, starting transfers between devices, ring(): blocks.append(lax.ppermute(ahead, 'z', up))  4.51 us
  transfers between devices with their start and end apart: 12, of which 7 were waited for; matrix products, arithmetic and copies ran while one was open for 0% of the time, Pallas kernels for 1%

profile of v4, /device:TPU:1, one launch (start us, length us, event | category | flops | bytes accessed | tf_op | source)
XLA Modules:
  0.0 162.6 jit_solution(5148292296333170677)
XLA Ops:
  0.0 1.6 collective-permute-start.7
  1.6 0.0 collective-permute-done.7
  1.6 0.2 broadcast_in_dim.6
  1.8 0.0 copy-start
  1.8 0.0 copy-start.1
  1.8 40.9 %all_to_all.10.refs_8_ = f32[16,128,256]{2,1,0:T(8,128)S(1)} all-to-all(f32[16,128,256]{2,1,0:T(8,128)S(1)} %broadcast_in_dim.6), channel_id=1, replica_groups=mesh['z'=16,'x'=4,'c'=2,'y'=4] {'x','y'}, dimensions={0} | all-to-all | bytes 4194304 | tf_op jit(solution)/shard_map/all_to_all | solution.py:144
  42.7 5.1 %collective-permute-start.8 = (f32[16,128,256]{2,1,0:T(8,128)S(1)}, f32[16,128,256]{2,1,0:T(8,128)S(1)}, u32[]{:S(2)}, u32[]{:S(2)}) collective-permute-start(f32[16,128,256]{2,1,0:T(8,128)S(1)} %all_to_all.10.refs_8_), channel_id=1, source_target_pairs={{0,4},{4,0},{1,5},{5,1},{2,6},{6,2},{3,7},{7,3},{8,12},{12,8},{9,1... | collective-permute-start | bytes 6291464 | tf_op jit(solution)/shard_map/ppermute | solution.py:162
  47.8 0.0 copy-done
  47.8 4.9 %collective-permute-start = (f32[128,256]{1,0:T(8,128)S(1)}, f32[128,256]{1,0:T(8,128)S(1)}, u32[]{:S(2)}, u32[]{:S(2)}) collective-permute-start(f32[128,256]{1,0:T(8,128)S(1)} %copy-done), channel_id=1, source_target_pairs={{0,64},{32,96},{64,128},{96,160},{128,192},{160,224},{192,256},{22... | collective-permute-start | bytes 393224 | tf_op jit(solution)/shard_map/ppermute | solution.py:132
  52.7 8.6 %collective-permute-start.1 = (f32[128,256]{1,0:T(8,128)S(1)}, f32[128,256]{1,0:T(8,128)S(1)}, u32[]{:S(2)}, u32[]{:S(2)}) collective-permute-start(f32[128,256]{1,0:T(8,128)S(1)} %copy-done), channel_id=1, source_target_pairs={{0,448},{32,480},{64,0},{96,32},{128,64},{160,96},{192,128},{224,1... | collective-permute-start | bytes 393224 | tf_op jit(solution)/shard_map/ppermute | solution.py:133
  61.3 4.8 %collective-permute-done.refs_1_ = f32[128,256]{1,0:T(8,128)S(1)} collective-permute-done((f32[128,256]{1,0:T(8,128)S(1)}, f32[128,256]{1,0:T(8,128)S(1)}, u32[]{:S(2)}, u32[]{:S(2)}) %collective-permute-start) | collective-permute-done | bytes 131104 | tf_op jit(solution)/shard_map/ppermute | solution.py:132
  66.1 1.9 %collective-permute-start.2 = (f32[128,256]{1,0:T(8,128)S(1)}, f32[128,256]{1,0:T(8,128)S(1)}, u32[]{:S(2)}, u32[]{:S(2)}) collective-permute-start(f32[128,256]{1,0:T(8,128)S(1)} %collective-permute-done.refs_1_), channel_id=1, source_target_pairs={{0,64},{32,96},{64,128},{96,160},{128,192},{160,224},{192,256},{22... | collective-permute-start | bytes 393224 | tf_op jit(solution)/shard_map/ppermute | solution.py:132
  68.1 0.0 collective-permute-done.1.refs_2_
  68.1 5.5 %collective-permute-start.3 = (f32[128,256]{1,0:T(8,128)S(1)}, f32[128,256]{1,0:T(8,128)S(1)}, u32[]{:S(2)}, u32[]{:S(2)}) collective-permute-start(f32[128,256]{1,0:T(8,128)S(1)} %collective-permute-done.1.refs_2_), channel_id=1, source_target_pairs={{0,448},{32,480},{64,0},{96,32},{128,64},{160,96},{192,128},{224,1... | collective-permute-start | bytes 393224 | tf_op jit(solution)/shard_map/ppermute | solution.py:133
  73.5 1.1 collective-permute-done.2.refs_3_
  74.7 2.8 %collective-permute-start.4 = (f32[128,256]{1,0:T(8,128)S(1)}, f32[128,256]{1,0:T(8,128)S(1)}, u32[]{:S(2)}, u32[]{:S(2)}) collective-permute-start(f32[128,256]{1,0:T(8,128)S(1)} %collective-permute-done.2.refs_3_), channel_id=1, source_target_pairs={{0,64},{32,96},{64,128},{96,160},{128,192},{160,224},{192,256},{22... | collective-permute-start | bytes 393224 | tf_op jit(solution)/shard_map/ppermute | solution.py:132
  77.5 0.0 collective-permute-done.3.refs_4_
  77.5 4.5 %collective-permute-start.5 = (f32[128,256]{1,0:T(8,128)S(1)}, f32[128,256]{1,0:T(8,128)S(1)}, u32[]{:S(2)}, u32[]{:S(2)}) collective-permute-start(f32[128,256]{1,0:T(8,128)S(1)} %collective-permute-done.3.refs_4_), channel_id=1, source_target_pairs={{0,448},{32,480},{64,0},{96,32},{128,64},{160,96},{192,128},{224,1... | collective-permute-start | bytes 393224 | tf_op jit(solution)/shard_map/ppermute | solution.py:133
  82.1 0.5 collective-permute-done.4.refs_5_
  82.6 4.5 %collective-permute-start.6 = (f32[128,256]{1,0:T(8,128)S(1)}, f32[128,256]{1,0:T(8,128)S(1)}, u32[]{:S(2)}, u32[]{:S(2)}) collective-permute-start(f32[128,256]{1,0:T(8,128)S(1)} %collective-permute-done.4.refs_5_), channel_id=1, source_target_pairs={{0,64},{32,96},{64,128},{96,160},{128,192},{160,224},{192,256},{22... | collective-permute-start | bytes 393224 | tf_op jit(solution)/shard_map/ppermute | solution.py:135
  87.1 0.0 copy-done.1
  87.1 0.2 broadcast_in_dim.7
  87.3 0.3 copy.5
  87.6 0.8 collective-permute-done.5.refs_6_
  88.4 3.0 %collective-permute-done.6.refs_7_ = f32[128,256]{1,0:T(8,128)S(1)} collective-permute-done((f32[128,256]{1,0:T(8,128)S(1)}, f32[128,256]{1,0:T(8,128)S(1)}, u32[]{:S(2)}, u32[]{:S(2)}) %collective-permute-start.6) | collective-permute-done | bytes 131104 | tf_op jit(solution)/shard_map/ppermute | solution.py:135
  91.4 0.8 shard_map.28
  92.1 0.0 collective-permute-done.8.other_ref
  92.1 0.4 shard_map.30
  92.6 4.6 %collective-permute-start.9 = (f32[128,256]{1,0:T(8,128)S(1)}, f32[128,256]{1,0:T(8,128)S(1)}, u32[]{:S(2)}, u32[]{:S(2)}) collective-permute-start(f32[128,256]{1,0:T(8,128)S(1)} %shard_map.30), channel_id=1, source_target_pairs={{0,32},{32,0},{64,96},{96,64},{128,160},{160,128},{192,224},{224,1... | collective-permute-start | bytes 393224 | tf_op jit(solution)/shard_map/ppermute | solution.py:168
  97.2 0.4 shard_map.29
  97.6 1.9 %collective-permute-done.9 = f32[128,256]{1,0:T(8,128)S(1)} collective-permute-done((f32[128,256]{1,0:T(8,128)S(1)}, f32[128,256]{1,0:T(8,128)S(1)}, u32[]{:S(2)}, u32[]{:S(2)}) %collective-permute-start.9) | collective-permute-done | bytes 131104 | tf_op jit(solution)/shard_map/ppermute | solution.py:168
  99.6 0.2 broadcast_in_dim.8
  99.8 27.3 %all_to_all.11.mine_ref = f32[16,128,256]{2,1,0:T(8,128)S(1)} all-to-all(f32[16,128,256]{2,1,0:T(8,128)S(1)} %broadcast_in_dim.8), channel_id=1, replica_groups=mesh['z'=16,'x'=4,'c'=2,'y'=4] {'x','y'}, dimensions={0} | all-to-all | bytes 4194304 | tf_op jit(solution)/shard_map/all_to_all | solution.py:144
  127.0 6.7 %collective-permute-start.11 = (f32[16,128,256]{2,1,0:T(8,128)S(1)}, f32[16,128,256]{2,1,0:T(8,128)S(1)}, u32[]{:S(2)}, u32[]{:S(2)}) collective-permute-start(f32[16,128,256]{2,1,0:T(8,128)S(1)} %all_to_all.11.mine_ref), channel_id=1, source_target_pairs={{0,4},{4,0},{1,5},{5,1},{2,6},{6,2},{3,7},{7,3},{8,12},{12,8},{9,1... | collective-permute-start | bytes 6291464 | tf_op jit(solution)/shard_map/ppermute | solution.py:171
  133.8 3.5 %collective-permute-start.10 = (f32[8,128,256]{2,1,0:T(8,128)S(1)}, f32[8,128,256]{2,1,0:T(8,128)S(1)}, u32[]{:S(2)}, u32[]{:S(2)}) collective-permute-start(f32[8,128,256]{2,1,0:T(8,128)S(1)} %get-tuple-element.8.panel_ref.here_ref), channel_id=1, source_target_pairs={{0,32},{32,0},{64,96},{96,64},{128,160},{160,128},{192,224},{224,1... | collective-permute-start | bytes 3145736 | tf_op jit(solution)/shard_map/ppermute | solution.py:169
  137.3 23.4 %collective-permute-done.10.there_ref = f32[8,128,256]{2,1,0:T(8,128)S(1)} collective-permute-done((f32[8,128,256]{2,1,0:T(8,128)S(1)}, f32[8,128,256]{2,1,0:T(8,128)S(1)}, u32[]{:S(2)}, u32[]{:S(2)}) %collective-permute-start.10) | collective-permute-done | bytes 1048608 | tf_op jit(solution)/shard_map/ppermute | solution.py:169
  160.7 0.6 shard_map.31.start_ref
  161.3 0.0 collective-permute-done.11.other_ref
  161.3 1.3 shard_map.32
  (2 shorter events, 0.0 us)
Async XLA Ops:
  0.0 1.6 collective-permute-start.7
  1.8 46.1 %copy-start = (f32[128,256]{1,0:T(8,128)S(1)}, f32[128,256]{1,0:T(8,128)}, u32[]{:S(2)}) copy-start(f32[128,256]{1,0:T(8,128)} %refs_0_.1) | copy-start | bytes 393220
  1.8 85.3 %copy-start.1 = (s32[32,32]{1,0:T(8,128)S(1)}, s32[32,32]{1,0:T(8,128)}, u32[]{:S(2)}) copy-start(s32[32,32]{1,0:T(8,128)} %param.3) | copy-start | bytes 12292
  42.7 49.5 %collective-permute-start.8 = (f32[16,128,256]{2,1,0:T(8,128)S(1)}, f32[16,128,256]{2,1,0:T(8,128)S(1)}, u32[]{:S(2)}, u32[]{:S(2)}) collective-permute-start(f32[16,128,256]{2,1,0:T(8,128)S(1)} %all_to_all.10.refs_8_), channel_id=1, source_target_pairs={{0,4},{4,0},{1,5},{5,1},{2,6},{6,2},{3,7},{7,3},{8,12},{12,8},{9,1... | collective-permute-start | bytes 6291464 | tf_op jit(solution)/shard_map/ppermute | solution.py:162
  47.8 18.3 %collective-permute-start = (f32[128,256]{1,0:T(8,128)S(1)}, f32[128,256]{1,0:T(8,128)S(1)}, u32[]{:S(2)}, u32[]{:S(2)}) collective-permute-start(f32[128,256]{1,0:T(8,128)S(1)} %copy-done), channel_id=1, source_target_pairs={{0,64},{32,96},{64,128},{96,160},{128,192},{160,224},{192,256},{22... | collective-permute-start | bytes 393224 | tf_op jit(solution)/shard_map/ppermute | solution.py:132
  52.7 15.3 %collective-permute-start.1 = (f32[128,256]{1,0:T(8,128)S(1)}, f32[128,256]{1,0:T(8,128)S(1)}, u32[]{:S(2)}, u32[]{:S(2)}) collective-permute-start(f32[128,256]{1,0:T(8,128)S(1)} %copy-done), channel_id=1, source_target_pairs={{0,448},{32,480},{64,0},{96,32},{128,64},{160,96},{192,128},{224,1... | collective-permute-start | bytes 393224 | tf_op jit(solution)/shard_map/ppermute | solution.py:133
  66.1 8.5 %collective-permute-start.2 = (f32[128,256]{1,0:T(8,128)S(1)}, f32[128,256]{1,0:T(8,128)S(1)}, u32[]{:S(2)}, u32[]{:S(2)}) collective-permute-start(f32[128,256]{1,0:T(8,128)S(1)} %collective-permute-done.refs_1_), channel_id=1, source_target_pairs={{0,64},{32,96},{64,128},{96,160},{128,192},{160,224},{192,256},{22... | collective-permute-start | bytes 393224 | tf_op jit(solution)/shard_map/ppermute | solution.py:132
  68.1 9.5 %collective-permute-start.3 = (f32[128,256]{1,0:T(8,128)S(1)}, f32[128,256]{1,0:T(8,128)S(1)}, u32[]{:S(2)}, u32[]{:S(2)}) collective-permute-start(f32[128,256]{1,0:T(8,128)S(1)} %collective-permute-done.1.refs_2_), channel_id=1, source_target_pairs={{0,448},{32,480},{64,0},{96,32},{128,64},{160,96},{192,128},{224,1... | collective-permute-start | bytes 393224 | tf_op jit(solution)/shard_map/ppermute | solution.py:133
  74.7 7.9 %collective-permute-start.4 = (f32[128,256]{1,0:T(8,128)S(1)}, f32[128,256]{1,0:T(8,128)S(1)}, u32[]{:S(2)}, u32[]{:S(2)}) collective-permute-start(f32[128,256]{1,0:T(8,128)S(1)} %collective-permute-done.2.refs_3_), channel_id=1, source_target_pairs={{0,64},{32,96},{64,128},{96,160},{128,192},{160,224},{192,256},{22... | collective-permute-start | bytes 393224 | tf_op jit(solution)/shard_map/ppermute | solution.py:132
  77.5 10.9 %collective-permute-start.5 = (f32[128,256]{1,0:T(8,128)S(1)}, f32[128,256]{1,0:T(8,128)S(1)}, u32[]{:S(2)}, u32[]{:S(2)}) collective-permute-start(f32[128,256]{1,0:T(8,128)S(1)} %collective-permute-done.3.refs_4_), channel_id=1, source_target_pairs={{0,448},{32,480},{64,0},{96,32},{128,64},{160,96},{192,128},{224,1... | collective-permute-start | bytes 393224 | tf_op jit(solution)/shard_map/ppermute | solution.py:133
  82.6 8.8 %collective-permute-start.6 = (f32[128,256]{1,0:T(8,128)S(1)}, f32[128,256]{1,0:T(8,128)S(1)}, u32[]{:S(2)}, u32[]{:S(2)}) collective-permute-start(f32[128,256]{1,0:T(8,128)S(1)} %collective-permute-done.4.refs_5_), channel_id=1, source_target_pairs={{0,64},{32,96},{64,128},{96,160},{128,192},{160,224},{192,256},{22... | collective-permute-start | bytes 393224 | tf_op jit(solution)/shard_map/ppermute | solution.py:135
  92.6 7.0 %collective-permute-start.9 = (f32[128,256]{1,0:T(8,128)S(1)}, f32[128,256]{1,0:T(8,128)S(1)}, u32[]{:S(2)}, u32[]{:S(2)}) collective-permute-start(f32[128,256]{1,0:T(8,128)S(1)} %shard_map.30), channel_id=1, source_target_pairs={{0,32},{32,0},{64,96},{96,64},{128,160},{160,128},{192,224},{224,1... | collective-permute-start | bytes 393224 | tf_op jit(solution)/shard_map/ppermute | solution.py:168
  127.0 34.3 %collective-permute-start.11 = (f32[16,128,256]{2,1,0:T(8,128)S(1)}, f32[16,128,256]{2,1,0:T(8,128)S(1)}, u32[]{:S(2)}, u32[]{:S(2)}) collective-permute-start(f32[16,128,256]{2,1,0:T(8,128)S(1)} %all_to_all.11.mine_ref), channel_id=1, source_target_pairs={{0,4},{4,0},{1,5},{5,1},{2,6},{6,2},{3,7},{7,3},{8,12},{12,8},{9,1... | collective-permute-start | bytes 6291464 | tf_op jit(solution)/shard_map/ppermute | solution.py:171
  133.8 26.9 %collective-permute-start.10 = (f32[8,128,256]{2,1,0:T(8,128)S(1)}, f32[8,128,256]{2,1,0:T(8,128)S(1)}, u32[]{:S(2)}, u32[]{:S(2)}) collective-permute-start(f32[8,128,256]{2,1,0:T(8,128)S(1)} %get-tuple-element.8.panel_ref.here_ref), channel_id=1, source_target_pairs={{0,32},{32,0},{64,96},{96,64},{128,160},{160,128},{192,224},{224,1... | collective-permute-start | bytes 3145736 | tf_op jit(solution)/shard_map/ppermute | solution.py:169
